TPU v7x, 256 devices: a whole 4x4x8 slice. The times are simulated.
256 devices in a mesh: seq: 64 (over z_hi, x, y), head: 4 (over z_lo, core).
Axes of the slice: x: 4, y: 4, z: 8 (z_hi: 4, z_lo: 2; z = z_hi * 2 + z_lo), core: 2. Of those that a mesh axis runs over, the one named last changes fastest.
Arguments:
- q_tokens: bfloat16 [16384, 4096], P(('seq', 'head')), may hold values from -6 to 6
- k_tokens: bfloat16 [16384, 4096], P(('seq', 'head')), may hold values from -6 to 6
- v_tokens: bfloat16 [16384, 4096], P(('seq', 'head')), may hold values from -4 to 4
- grad_out: bfloat16 [16384, 4096], P(('seq', 'head')), may hold values from -4 to 4
- block_lists: int32 [256, 3], P('seq'), may hold values from 0 to 3, as said below
- block_valid: int32 [256, 3], P('seq'), may hold values from 0 to 1, as said below
Outputs:
- attended: bfloat16 [16384, 4096], P(('seq', 'head'))
- grad_q: bfloat16 [16384, 4096], P('seq', 'head')
- grad_k: bfloat16 [16384, 4096], P('seq', 'head')
- grad_v: bfloat16 [16384, 4096], P('seq', 'head')
Inputs may be any that keep to these rules, and one draw needn't show every extreme that they name: `block_lists`: among the 4 entries of one level of the query blocks of one span of 256 tokens, exactly 2 distinct values appear. `block_valid`: entry e of query block b is 0 wherever b // 4 < 2 * 4^e.
All inputs are finite; a program needn't handle non-finite values.
Results may differ from a plain program's by a relative error of at most 0.022.
Values may be sent and summed in bfloat16 or wider, within the bound.
No kernel may reach another device: no remote copies, remote signals or barrier semaphores. Data moves between devices by JAX's collectives and lax.ppermute only.
A program may use at most 128 MiB of HBM per device.

v0:
```python
import jax
import jax.numpy as jnp
from jax import lax
from jax.sharding import PartitionSpec as P

HEAD_DIM = 128
WINDOW = 256
BLOCK = 64
LEVELS = 3


NEG = -1e30


def passed_along(shard, axis, by):
    peers = lax.axis_size(axis)
    pairs = [(i, i + by) for i in range(peers) if 0 <= i + by < peers]
    return lax.ppermute(shard, axis, pairs)


def per_device(q_tokens, k_tokens, v_tokens, grad_out, block_lists, block_valid):
    query_rows, key_rows, value_rows, cotan_rows = (
        lax.all_to_all(q_tokens, "head", split_axis=1, concat_axis=0, tiled=True),
        lax.all_to_all(k_tokens, "head", split_axis=1, concat_axis=0, tiled=True),
        lax.all_to_all(v_tokens, "head", split_axis=1, concat_axis=0, tiled=True),
        lax.all_to_all(grad_out, "head", split_axis=1, concat_axis=0, tiled=True),
    )
    span_tokens = query_rows.shape[0]
    feature_cols = query_rows.shape[1]
    head_count = feature_cols // HEAD_DIM
    block_count = span_tokens // BLOCK
    score_scale = HEAD_DIM ** (-0.5)
    cycle_size = lax.axis_size("seq")
    start = lax.axis_index("seq") * span_tokens
    prev_keys, prev_values = passed_along((key_rows, value_rows), "seq", 1)
    key_win = jnp.concatenate([prev_keys, key_rows], 0).reshape(
        WINDOW + span_tokens, head_count, HEAD_DIM
    )
    value_win = jnp.concatenate([prev_values, value_rows], 0).reshape(
        WINDOW + span_tokens, head_count, HEAD_DIM
    )
    query_heads = query_rows.reshape(span_tokens, head_count, HEAD_DIM)
    cotan_heads = cotan_rows.reshape(span_tokens, head_count, HEAD_DIM)
    key_blocks = key_rows.reshape(block_count, BLOCK, feature_cols)
    value_blocks = value_rows.reshape(block_count, BLOCK, feature_cols)
    reached = [reach_level for reach_level in range(LEVELS) if 2 * 4**reach_level < cycle_size]
    slot_rows = {}
    far_keys = {}
    far_values = {}
    for reach_level in reached:
        distance = 2 * 4**reach_level
        picks = block_lists[:, reach_level]
        got_keys, got_values = passed_along((key_blocks, value_blocks), "seq", distance)
        slot_rows[reach_level] = picks
        far_keys[reach_level] = got_keys
        far_values[reach_level] = got_values
    level_total = len(reached)
    key_far = jnp.stack(
        [
            jnp.take(far_keys[reach_level], slot_rows[reach_level], axis=0)
            for reach_level in reached
        ],
        1,
    )
    value_far = jnp.stack(
        [
            jnp.take(far_values[reach_level], slot_rows[reach_level], axis=0)
            for reach_level in reached
        ],
        1,
    )
    key_far = key_far.reshape(block_count, level_total * BLOCK, head_count, HEAD_DIM)
    value_far = value_far.reshape(block_count, level_total * BLOCK, head_count, HEAD_DIM)
    live_rows = jnp.stack([block_valid[:, reach_level] for reach_level in reached], 1)
    query_pos = start + jnp.arange(span_tokens, dtype=jnp.int32)
    key_pos = start - WINDOW + jnp.arange(WINDOW + span_tokens, dtype=jnp.int32)
    near_mask = (
        (key_pos[None, :] <= query_pos[:, None])
        & (key_pos[None, :] > query_pos[:, None] - WINDOW)
        & (key_pos[None, :] >= 0)
    )
    score_win = (
        jnp.einsum("thd,jhd->htj", query_heads, key_win, preferred_element_type=jnp.float32)
        * score_scale
    )
    score_win = jnp.where(near_mask[None], score_win, NEG)
    query_blk = query_heads.reshape(block_count, BLOCK, head_count, HEAD_DIM)
    cotan_blk = cotan_heads.reshape(block_count, BLOCK, head_count, HEAD_DIM)
    far_mask = jnp.repeat(live_rows > 0, BLOCK, axis=1)
    score_far = (
        jnp.einsum("bqhd,bkhd->hbqk", query_blk, key_far, preferred_element_type=jnp.float32)
        * score_scale
    )
    score_far = jnp.where(far_mask[None, :, None, :], score_far, NEG)
    row_top = jnp.maximum(
        jnp.max(score_win, -1), jnp.max(score_far, -1).reshape(head_count, span_tokens)
    )
    row_total = jnp.sum(jnp.exp(score_win - row_top[..., None]), -1)
    row_total = row_total + jnp.sum(
        jnp.exp(score_far - row_top.reshape(head_count, block_count, BLOCK)[..., None]), -1
    ).reshape(head_count, span_tokens)
    log_total = row_top + jnp.log(row_total)
    weight_win = jnp.exp(score_win - log_total[..., None])
    weight_far = jnp.exp(score_far - log_total.reshape(head_count, block_count, BLOCK)[..., None])
    weight_win_b = weight_win.astype(jnp.bfloat16)
    weight_far_b = weight_far.astype(jnp.bfloat16)
    attended_f = jnp.einsum(
        "htj,jhd->thd", weight_win_b, value_win, preferred_element_type=jnp.float32
    )
    attended_f = attended_f + jnp.einsum(
        "hbqk,bkhd->bqhd", weight_far_b, value_far, preferred_element_type=jnp.float32
    ).reshape(span_tokens, head_count, HEAD_DIM)
    attended_b = attended_f.astype(jnp.bfloat16)
    attended = lax.all_to_all(
        attended_b.reshape(span_tokens, feature_cols),
        "head",
        split_axis=0,
        concat_axis=1,
        tiled=True,
    )
    delta = jnp.einsum("thd,thd->ht", cotan_heads, attended_b, preferred_element_type=jnp.float32)
    dprob_win = jnp.einsum(
        "thd,jhd->htj", cotan_heads, value_win, preferred_element_type=jnp.float32
    )
    dscore_win_b = (weight_win * (dprob_win - delta[..., None])).astype(jnp.bfloat16)
    dprob_far = jnp.einsum(
        "bqhd,bkhd->hbqk", cotan_blk, value_far, preferred_element_type=jnp.float32
    )
    dscore_far_b = (
        weight_far * (dprob_far - delta.reshape(head_count, block_count, BLOCK)[..., None])
    ).astype(jnp.bfloat16)
    query_grad = jnp.einsum(
        "htj,jhd->thd", dscore_win_b, key_win, preferred_element_type=jnp.float32
    )
    query_grad = query_grad + jnp.einsum(
        "hbqk,bkhd->bqhd", dscore_far_b, key_far, preferred_element_type=jnp.float32
    ).reshape(span_tokens, head_count, HEAD_DIM)
    grad_q = (score_scale * query_grad).reshape(span_tokens, feature_cols).astype(jnp.bfloat16)
    key_grad_win = (
        score_scale
        * jnp.einsum("htj,thd->jhd", dscore_win_b, query_heads, preferred_element_type=jnp.float32)
    ).reshape(WINDOW + span_tokens, feature_cols)
    value_grad_win = jnp.einsum(
        "htj,thd->jhd", weight_win_b, cotan_heads, preferred_element_type=jnp.float32
    ).reshape(WINDOW + span_tokens, feature_cols)
    key_grad_far = (
        score_scale
        * jnp.einsum("hbqk,bqhd->bkhd", dscore_far_b, query_blk, preferred_element_type=jnp.float32)
    ).reshape(block_count, level_total, BLOCK, feature_cols)
    value_grad_far = jnp.einsum(
        "hbqk,bqhd->bkhd", weight_far_b, cotan_blk, preferred_element_type=jnp.float32
    ).reshape(block_count, level_total, BLOCK, feature_cols)
    back_keys, back_values = passed_along(
        (key_grad_win[:WINDOW], value_grad_win[:WINDOW]), "seq", -1
    )
    key_total = (
        key_grad_win[WINDOW:]
        .at[span_tokens - WINDOW :]
        .add(back_keys)
        .reshape(block_count, BLOCK, feature_cols)
    )
    value_total = (
        value_grad_win[WINDOW:]
        .at[span_tokens - WINDOW :]
        .add(back_values)
        .reshape(block_count, BLOCK, feature_cols)
    )
    for reach_level in reached:
        distance = 2 * 4**reach_level
        position = reached.index(reach_level)
        slot_total = far_keys[reach_level].shape[0]
        spread = (
            slot_rows[reach_level][:, None] == jnp.arange(slot_total, dtype=jnp.int32)[None, :]
        ).astype(jnp.float32)
        summed_keys = jnp.einsum(
            "bs,btc->stc", spread, key_grad_far[:, position], precision=lax.Precision.HIGHEST
        )
        summed_values = jnp.einsum(
            "bs,btc->stc", spread, value_grad_far[:, position], precision=lax.Precision.HIGHEST
        )
        return_keys, return_values = passed_along((summed_keys, summed_values), "seq", -distance)
        key_total = key_total + return_keys
        value_total = value_total + return_values
    grad_k = key_total.reshape(span_tokens, feature_cols).astype(jnp.bfloat16)
    grad_v = value_total.reshape(span_tokens, feature_cols).astype(jnp.bfloat16)
    return (attended, grad_q, grad_k, grad_v)


def solution(mesh):
    in_specs = (
        P(("seq", "head"), None),
        P(("seq", "head"), None),
        P(("seq", "head"), None),
        P(("seq", "head"), None),
        P("seq", None),
        P("seq", None),
    )
    out_specs = (P(("seq", "head"), None), P("seq", "head"), P("seq", "head"), P("seq", "head"))
    return jax.shard_map(
        per_device, mesh=mesh, in_specs=in_specs, out_specs=out_specs, check_vma=False
    )
```

profile of v0, /device:TPU:32, one launch (start us, length us, event | category | flops | bytes accessed | tf_op | source)
XLA Modules:
  0.0 673.5 jit_solution(17683482233335155028)
XLA Ops:
  2.6 5.4 all-to-all-start.2
  8.8 6.3 all-to-all-done.2
  15.2 5.7 all-to-all-start.1
  22.0 6.2 all-to-all-done.1
  28.2 5.7 all-to-all-start
  36.8 4.4 all-to-all-done
  41.2 5.1 all-to-all-start.4
  46.3 3.4 collective-permute-start.5
  49.7 5.7 collective-permute-start.6
  55.5 9.0 %collective-permute-start.7 = (bf16[4,64,1024]{2,1,0:T(8,128)(2,1)}, bf16[4,64,1024]{2,1,0:T(8,128)(2,1)}, u32[]{:S(2)}, u32[]{:S(2)}) collective-permute-start(bf16[4,64,1024]{2,1,0:T(8,128)(2,1)} %bitcast.2), channel_id=1, source_target_pairs={{0,128},{4,132},{8,136},{12,140},{16,144},{20,148},{24,152},{28,15... | collective-permute-start | bytes 1572872 | tf_op jit(solution)/shard_map/ppermute | solution.py:18
  64.5 3.7 collective-permute-start.2
  68.2 3.7 collective-permute-start.3
  80.1 63.4 %collective-permute-start.4 = (bf16[4,64,1024]{2,1,0:T(8,128)(2,1)}, bf16[4,64,1024]{2,1,0:T(8,128)(2,1)}, u32[]{:S(2)}, u32[]{:S(2)}) collective-permute-start(bf16[4,64,1024]{2,1,0:T(8,128)(2,1)} %bitcast.5), channel_id=1, source_target_pairs={{0,128},{4,132},{8,136},{12,140},{16,144},{20,148},{24,152},{28,15... | collective-permute-start | bytes 1572872 | tf_op jit(solution)/shard_map/ppermute | solution.py:18
  144.1 20.1 %collective-permute-start = (bf16[256,1024]{1,0:T(8,128)(2,1)}, bf16[256,1024]{1,0:T(8,128)(2,1)}, u32[]{:S(2)}, u32[]{:S(2)}) collective-permute-start(bf16[256,1024]{1,0:T(8,128)(2,1)} %bitcast.3), channel_id=1, source_target_pairs={{0,4},{4,8},{8,12},{12,16},{16,20},{20,24},{24,28},{28,32},{32,36}... | collective-permute-start | bytes 1572872 | tf_op jit(solution)/shard_map/ppermute | solution.py:18
  165.8 2.4 gather_fusion.4
  168.2 2.4 gather_fusion.1
  170.7 2.4 gather_fusion.5
  174.5 2.4 gather_fusion.2
  182.2 4.1 fusion.2
  187.2 3.1 exponential_reduce_fusion
  190.3 2.1 fusion.14
  194.1 2.6 copy.163
  198.7 5.1 bitcast_convert_fusion
  203.8 2.6 copy.211
  208.1 5.6 fusion
  213.8 2.6 convolution_bitcast_fusion.1
  217.9 3.5 copy.219
  221.4 4.9 reshape.364
  226.3 3.3 fusion.25
  229.6 3.4 fusion.26
  233.0 3.3 fusion.27
  238.5 3.5 copy.217
  242.0 3.1 reshape.363
  245.1 2.1 fusion.28
  247.2 2.1 fusion.29
  249.3 2.1 copy.164
  253.4 4.3 all-to-all-start.3
  257.8 3.0 copy.202
  269.5 2.6 copy.193
  273.4 2.5 multiply_bitcast_fusion.1
  277.5 2.1 fusion.30
  279.5 2.7 copy.180
  288.5 3.7 collective-permute-done.14
  294.7 125.8 %collective-permute-done.15 = f32[4,64,1024]{2,1,0:T(8,128)} collective-permute-done((f32[4,64,1024]{2,1,0:T(8,128)}, f32[4,64,1024]{2,1,0:T(8,128)}, u32[]{:S(2)}, u32[]{:S(2)}) %collective-permute-start.15) | collective-permute-done | bytes 1048608 | tf_op jit(solution)/shard_map/ppermute | solution.py:18
  424.6 3.0 fusion.23
  433.3 3.4 add_convert_fusion
  436.7 233.1 %collective-permute-done.11 = f32[4,64,1024]{2,1,0:T(8,128)} collective-permute-done((f32[4,64,1024]{2,1,0:T(8,128)}, f32[4,64,1024]{2,1,0:T(8,128)}, u32[]{:S(2)}, u32[]{:S(2)}) %collective-permute-start.11) | collective-permute-done | bytes 1048608 | tf_op jit(solution)/shard_map/ppermute | solution.py:18
  669.8 3.4 add_convert_fusion.1
  (150 shorter events, 65.9 us)
Async XLA Ops:
  0.6 7.4 %copy-start.20 = (bf16[64,4096]{1,0:T(8,128)(2,1)S(1)}, bf16[64,4096]{1,0:T(8,128)(2,1)}, u32[]{:S(2)}) copy-start(bf16[64,4096]{1,0:T(8,128)(2,1)} %param.17) | copy-start | bytes 1572868
  0.6 20.3 %copy-start.23 = (s32[4,3]{1,0:T(4,128)S(1)}, s32[4,3]{1,0:T(4,128)}, u32[]{:S(2)}) copy-start(s32[4,3]{1,0:T(4,128)} %param.20) | copy-start | bytes 148
  0.7 20.5 %copy-start.21 = (bf16[64,4096]{1,0:T(8,128)(2,1)S(1)}, bf16[64,4096]{1,0:T(8,128)(2,1)}, u32[]{:S(2)}) copy-start(bf16[64,4096]{1,0:T(8,128)(2,1)} %param.18) | copy-start | bytes 1572868
  2.6 19.4 %copy-start.24 = (s32[4,3]{1,0:T(4,128)S(1)}, s32[4,3]{1,0:T(4,128)}, u32[]{:S(2)}) copy-start(s32[4,3]{1,0:T(4,128)} %param.21) | copy-start | bytes 148
  2.6 12.6 %all-to-all-start.2 = ((bf16[64,4,1024]{2,0,1:T(8,128)(2,1)}), bf16[64,4,1024]{2,0,1:T(8,128)(2,1)S(1)}, u32[]{:S(2)}, u32[]{:S(2)}) async-start(bf16[64,4,1024]{2,0,1:T(8,128)(2,1)} %bitcast.213), calls=%async_computation.2 | async-start | bytes 1048576 | tf_op jit(solution)/shard_map/all_to_all | solution.py:23
  8.0 26.1 %copy-start.22 = (bf16[64,4096]{1,0:T(8,128)(2,1)S(1)}, bf16[64,4096]{1,0:T(8,128)(2,1)}, u32[]{:S(2)}) copy-start(bf16[64,4096]{1,0:T(8,128)(2,1)} %param.19) | copy-start | bytes 1572868
  15.2 13.0 %all-to-all-start.1 = ((bf16[64,4,1024]{2,0,1:T(8,128)(2,1)}), bf16[64,4,1024]{2,0,1:T(8,128)(2,1)}, u32[]{:S(2)}, u32[]{:S(2)}) async-start(bf16[64,4,1024]{2,0,1:T(8,128)(2,1)} %bitcast.214), calls=%async_computation.1 | async-start | bytes 1048576 | tf_op jit(solution)/shard_map/all_to_all | solution.py:24
  28.2 13.0 %all-to-all-start = ((bf16[64,4,1024]{2,0,1:T(8,128)(2,1)}), bf16[64,4,1024]{2,0,1:T(8,128)(2,1)}, u32[]{:S(2)}, u32[]{:S(2)}) async-start(bf16[64,4,1024]{2,0,1:T(8,128)(2,1)} %bitcast.215), calls=%async_computation | async-start | bytes 1048576 | tf_op jit(solution)/shard_map/all_to_all | solution.py:25
  35.0 33.2 %collective-permute-start.1 = (bf16[256,1024]{1,0:T(8,128)(2,1)}, bf16[256,1024]{1,0:T(8,128)(2,1)S(1)}, u32[]{:S(2)}, u32[]{:S(2)}) collective-permute-start(bf16[256,1024]{1,0:T(8,128)(2,1)} %bitcast.6), channel_id=1, source_target_pairs={{0,4},{4,8},{8,12},{12,16},{16,20},{20,24},{24,28},{28,32},{32,36}... | collective-permute-start | bytes 1572872 | tf_op jit(solution)/shard_map/ppermute | solution.py:18
  41.2 36.4 %all-to-all-start.4 = ((bf16[64,4,1024]{2,0,1:T(8,128)(2,1)}), bf16[64,4,1024]{2,0,1:T(8,128)(2,1)S(1)}, u32[]{:S(2)}, u32[]{:S(2)}) async-start(bf16[64,4,1024]{2,0,1:T(8,128)(2,1)} %bitcast.212), calls=%async_computation.4 | async-start | bytes 1048576 | tf_op jit(solution)/shard_map/all_to_all | solution.py:26
  46.3 33.8 %collective-permute-start.5 = (bf16[4,64,1024]{2,1,0:T(8,128)(2,1)}, bf16[4,64,1024]{2,1,0:T(8,128)(2,1)S(1)}, u32[]{:S(2)}, u32[]{:S(2)}) collective-permute-start(bf16[4,64,1024]{2,1,0:T(8,128)(2,1)} %bitcast.2), channel_id=1, source_target_pairs={{0,8},{4,12},{8,16},{12,20},{16,24},{20,28},{24,32},{28,36},{32,40... | collective-permute-start | bytes 1572872 | tf_op jit(solution)/shard_map/ppermute | solution.py:18
  49.7 116.1 %collective-permute-start.6 = (bf16[4,64,1024]{2,1,0:T(8,128)(2,1)}, bf16[4,64,1024]{2,1,0:T(8,128)(2,1)}, u32[]{:S(2)}, u32[]{:S(2)}) collective-permute-start(bf16[4,64,1024]{2,1,0:T(8,128)(2,1)} %bitcast.2), channel_id=1, source_target_pairs={{0,32},{4,36},{8,40},{12,44},{16,48},{20,52},{24,56},{28,60},{32,6... | collective-permute-start | bytes 1572872 | tf_op jit(solution)/shard_map/ppermute | solution.py:18
  55.5 115.2 %collective-permute-start.7 = (bf16[4,64,1024]{2,1,0:T(8,128)(2,1)}, bf16[4,64,1024]{2,1,0:T(8,128)(2,1)}, u32[]{:S(2)}, u32[]{:S(2)}) collective-permute-start(bf16[4,64,1024]{2,1,0:T(8,128)(2,1)} %bitcast.2), channel_id=1, source_target_pairs={{0,128},{4,132},{8,136},{12,140},{16,144},{20,148},{24,152},{28,15... | collective-permute-start | bytes 1572872 | tf_op jit(solution)/shard_map/ppermute | solution.py:18
  64.5 79.6 %collective-permute-start.2 = (bf16[4,64,1024]{2,1,0:T(8,128)(2,1)}, bf16[4,64,1024]{2,1,0:T(8,128)(2,1)}, u32[]{:S(2)}, u32[]{:S(2)}) collective-permute-start(bf16[4,64,1024]{2,1,0:T(8,128)(2,1)} %bitcast.5), channel_id=1, source_target_pairs={{0,8},{4,12},{8,16},{12,20},{16,24},{20,28},{24,32},{28,36},{32,40... | collective-permute-start | bytes 1572872 | tf_op jit(solution)/shard_map/ppermute | solution.py:18
  68.2 100.0 %collective-permute-start.3 = (bf16[4,64,1024]{2,1,0:T(8,128)(2,1)}, bf16[4,64,1024]{2,1,0:T(8,128)(2,1)}, u32[]{:S(2)}, u32[]{:S(2)}) collective-permute-start(bf16[4,64,1024]{2,1,0:T(8,128)(2,1)} %bitcast.5), channel_id=1, source_target_pairs={{0,32},{4,36},{8,40},{12,44},{16,48},{20,52},{24,56},{28,60},{32,6... | collective-permute-start | bytes 1572872 | tf_op jit(solution)/shard_map/ppermute | solution.py:18
  77.7 2.5 copy-start.6
  80.1 94.3 %collective-permute-start.4 = (bf16[4,64,1024]{2,1,0:T(8,128)(2,1)}, bf16[4,64,1024]{2,1,0:T(8,128)(2,1)}, u32[]{:S(2)}, u32[]{:S(2)}) collective-permute-start(bf16[4,64,1024]{2,1,0:T(8,128)(2,1)} %bitcast.5), channel_id=1, source_target_pairs={{0,128},{4,132},{8,136},{12,140},{16,144},{20,148},{24,152},{28,15... | collective-permute-start | bytes 1572872 | tf_op jit(solution)/shard_map/ppermute | solution.py:18
  144.1 52.6 %collective-permute-start = (bf16[256,1024]{1,0:T(8,128)(2,1)}, bf16[256,1024]{1,0:T(8,128)(2,1)}, u32[]{:S(2)}, u32[]{:S(2)}) collective-permute-start(bf16[256,1024]{1,0:T(8,128)(2,1)} %bitcast.3), channel_id=1, source_target_pairs={{0,4},{4,8},{8,12},{12,16},{16,20},{20,24},{24,28},{28,32},{32,36}... | collective-permute-start | bytes 1572872 | tf_op jit(solution)/shard_map/ppermute | solution.py:18
  173.1 1.0 copy-start.17
  173.1 1.2 copy-start.18
  179.2 1.8 copy-start.3
  208.1 5.7 copy-start
  208.1 5.6 copy-start.19
  213.8 2.6 copy-start.7
  229.6 6.7 copy-start.5
  237.5 1.0 copy-start.13
  253.4 177.9 %all-to-all-start.3 = ((bf16[4,64,1024]{2,1,0:T(8,128)(2,1)}), bf16[4,64,1024]{2,1,0:T(8,128)(2,1)}, u32[]{:S(2)}, u32[]{:S(2)}) async-start(bf16[4,64,1024]{2,1,0:T(8,128)(2,1)} %all_to_all.77), calls=%async_computation.3 | async-start | bytes 1048576 | tf_op jit(solution)/shard_map/all_to_all | solution.py:114
  257.8 3.0 copy-start.11
  257.8 4.7 copy-start.10
  260.8 7.1 %copy-start.2 = (f32[512,8,128]{0,2,1:T(8,128)S(1)}, f32[512,8,128]{0,2,1:T(8,128)}, u32[]{:S(2)}) copy-start(f32[512,8,128]{0,2,1:T(8,128)} %convolution_bitcast_fusion.1) | copy-start | bytes 6291460
  264.1 28.1 %collective-permute-start.14 = (f32[4,64,1024]{2,1,0:T(8,128)}, f32[4,64,1024]{2,1,0:T(8,128)}, u32[]{:S(2)}, u32[]{:S(2)}) collective-permute-start(f32[4,64,1024]{2,1,0:T(8,128)} %copy.200), channel_id=1, source_target_pairs={{32,0},{36,4},{40,8},{44,12},{48,16},{52,20},{56,24},{60,28},{64,3... | collective-permute-start | bytes 3145736 | tf_op jit(solution)/shard_map/ppermute | solution.py:18
  265.4 28.1 %collective-permute-start.13 = (f32[4,64,1024]{2,1,0:T(8,128)}, f32[4,64,1024]{2,1,0:T(8,128)}, u32[]{:S(2)}, u32[]{:S(2)}) collective-permute-start(f32[4,64,1024]{2,1,0:T(8,128)} %copy.198), channel_id=1, source_target_pairs={{8,0},{12,4},{16,8},{20,12},{24,16},{28,20},{32,24},{36,28},{40,32... | collective-permute-start | bytes 3145736 | tf_op jit(solution)/shard_map/ppermute | solution.py:18
  266.7 153.9 %collective-permute-start.15 = (f32[4,64,1024]{2,1,0:T(8,128)}, f32[4,64,1024]{2,1,0:T(8,128)}, u32[]{:S(2)}, u32[]{:S(2)}) collective-permute-start(f32[4,64,1024]{2,1,0:T(8,128)} %copy.202), channel_id=1, source_target_pairs={{128,0},{132,4},{136,8},{140,12},{144,16},{148,20},{152,24},{156,2... | collective-permute-start | bytes 3145736 | tf_op jit(solution)/shard_map/ppermute | solution.py:18
  272.1 161.2 %collective-permute-start.12 = (f32[256,1024]{1,0:T(8,128)}, f32[256,1024]{1,0:T(8,128)}, u32[]{:S(2)}, u32[]{:S(2)}) collective-permute-start(f32[256,1024]{1,0:T(8,128)} %copy.193), channel_id=1, source_target_pairs={{4,0},{8,4},{12,8},{16,12},{20,16},{24,20},{28,24},{32,28},{36,32}... | collective-permute-start | bytes 3145736 | tf_op jit(solution)/shard_map/ppermute | solution.py:18
  279.5 4.1 copy-start.9
  279.5 5.7 copy-start.12
  282.2 4.6 copy-start.8
  282.2 154.5 %collective-permute-start.8 = (f32[256,1024]{1,0:T(8,128)}, f32[256,1024]{1,0:T(8,128)}, u32[]{:S(2)}, u32[]{:S(2)}) collective-permute-start(f32[256,1024]{1,0:T(8,128)} %copy.180), channel_id=1, source_target_pairs={{4,0},{8,4},{12,8},{16,12},{20,16},{24,20},{28,24},{32,28},{36,32}... | collective-permute-start | bytes 3145736 | tf_op jit(solution)/shard_map/ppermute | solution.py:18
  285.3 136.6 %copy-start.4 = (bf16[96,8,8,128]{3,2,1,0:T(8,128)(2,1)S(1)}, bf16[96,8,8,128]{3,2,1,0:T(8,128)(2,1)}, u32[]{:S(2)}) copy-start(bf16[96,8,8,128]{3,2,1,0:T(8,128)(2,1)} %copy-done.3) | copy-start | bytes 4718596
  285.3 136.6 %copy-start.14 = (bf16[8,4,64,192]{3,2,1,0:T(8,128)(2,1)S(1)}, bf16[8,4,64,192]{3,2,1,0:T(8,128)(2,1)}, u32[]{:S(2)}) copy-start(bf16[8,4,64,192]{3,2,1,0:T(8,128)(2,1)} %copy-done.13) | copy-start | bytes 2359300
  292.1 144.5 %collective-permute-start.10 = (f32[4,64,1024]{2,1,0:T(8,128)}, f32[4,64,1024]{2,1,0:T(8,128)}, u32[]{:S(2)}, u32[]{:S(2)}) collective-permute-start(f32[4,64,1024]{2,1,0:T(8,128)} %copy.187), channel_id=1, source_target_pairs={{32,0},{36,4},{40,8},{44,12},{48,16},{52,20},{56,24},{60,28},{64,3... | collective-permute-start | bytes 3145736 | tf_op jit(solution)/shard_map/ppermute | solution.py:18
  293.4 143.3 %collective-permute-start.9 = (f32[4,64,1024]{2,1,0:T(8,128)}, f32[4,64,1024]{2,1,0:T(8,128)}, u32[]{:S(2)}, u32[]{:S(2)}) collective-permute-start(f32[4,64,1024]{2,1,0:T(8,128)} %copy.185), channel_id=1, source_target_pairs={{8,0},{12,4},{16,8},{20,12},{24,16},{28,20},{32,24},{36,28},{40,32... | collective-permute-start | bytes 3145736 | tf_op jit(solution)/shard_map/ppermute | solution.py:18
  420.6 249.3 %collective-permute-start.11 = (f32[4,64,1024]{2,1,0:T(8,128)}, f32[4,64,1024]{2,1,0:T(8,128)}, u32[]{:S(2)}, u32[]{:S(2)}) collective-permute-start(f32[4,64,1024]{2,1,0:T(8,128)} %copy.189), channel_id=1, source_target_pairs={{128,0},{132,4},{136,8},{140,12},{144,16},{148,20},{152,24},{156,2... | collective-permute-start | bytes 3145736 | tf_op jit(solution)/shard_map/ppermute | solution.py:18
  422.6 2.0 copy-start.1
  424.6 5.0 copy-start.15
  429.6 1.2 copy-start.16
where the time goes:
time: 679 us; the launch traced here: 673 us
  waiting for transfers between devices  380 us (56%)
  starting transfers between devices  147 us (22%)
  local copies, waits for them, and re-layouts  83.9 us (12%)
  matrix products  46.5 us (7%)
  other arithmetic  14.5 us (2%)
    ppermute x16, waiting for transfers between devices, passed_along(): return lax.ppermute(shard, axis, pairs)  363 us
    ppermute x16, starting transfers between devices, passed_along(): return lax.ppermute(shard, axis, pairs)  121 us
  transfers between devices with their start and end apart: 21, of which 6 were waited for; matrix products, arithmetic and copies ran while one was open for 12% of the time, Pallas kernels for 0%

commit v1 on v0

v1 whole, which is shorter than its diff:
```python
import jax
import jax.numpy as jnp
from jax import lax
from jax.experimental import pallas as pl
from jax.experimental.pallas import tpu as pltpu
from jax.sharding import PartitionSpec as P

HEAD_DIM = 128
WINDOW = 256
BLOCK = 64
LEVELS = 3
NEG = -1e30


def passed_along(shard, by):
    peers = lax.axis_size("seq")
    pairs = [(i, i + by) for i in range(peers) if 0 <= i + by < peers]
    return lax.ppermute(shard, "seq", pairs)


def pack_body(a_ref, b_ref, out_ref):
    out_ref[0, 0] = a_ref[...]
    out_ref[0, 1] = b_ref[...]


def pack_pair(a, b, parts):
    rows, cols = a.shape
    piece = pl.BlockSpec((rows, cols // parts), lambda i: (0, i))
    return pl.pallas_call(
        pack_body,
        out_shape=jax.ShapeDtypeStruct((parts, 2, rows, cols // parts), a.dtype),
        grid=(parts,),
        in_specs=[piece, piece],
        out_specs=pl.BlockSpec((1, 2, rows, cols // parts), lambda i: (i, 0, 0, 0)),
        name="pack_pair",
    )(a, b)


def pick_body(idx_ref, kv_ref, *rest):
    outs, sems = rest[:-1], rest[-1]
    copies = []
    for level in reversed(range(LEVELS)):
        for slot in range(2):
            copies.append(
                pltpu.make_async_copy(
                    kv_ref.at[idx_ref[level, slot]], outs[level].at[slot], sems.at[level, slot]
                )
            )
    for copy in copies:
        copy.start()
    for copy in copies:
        copy.wait()


def pick_blocks(idx, kv):
    shape = jax.ShapeDtypeStruct((2,) + kv.shape[1:], kv.dtype)
    return pl.pallas_call(
        pick_body,
        out_shape=[shape] * LEVELS,
        grid_spec=pltpu.PrefetchScalarGridSpec(
            num_scalar_prefetch=1,
            in_specs=[pl.BlockSpec(memory_space=pltpu.VMEM)],
            out_specs=[pl.BlockSpec(memory_space=pl.ANY)] * LEVELS,
            grid=(1,),
            scratch_shapes=[pltpu.SemaphoreType.DMA((LEVELS, 2))],
        ),
        name="pick_blocks",
    )(idx, kv)


def dot_nt(a, b):
    return lax.dot_general(a, b, (((1,), (1,)), ((), ())), preferred_element_type=jnp.float32)


def dot_nn(a, b):
    return lax.dot_general(a, b, (((1,), (0,)), ((), ())), preferred_element_type=jnp.float32)


def dot_tn(a, b):
    return lax.dot_general(a, b, (((0,), (0,)), ((), ())), preferred_element_type=jnp.float32)


def attend_body(
    span_ref, lists_ref, valid_ref, used_ref,
    qd_ref, own_ref, prev_ref, far0_ref, far1_ref, far2_ref,
    att_ref, gq_ref, gown_ref, gprev_ref, gfar0_ref, gfar1_ref, gfar2_ref,
    bias_ref, k_ref, v_ref,
):
    rows = 4 * BLOCK
    near = WINDOW + rows
    scale = HEAD_DIM ** -0.5

    @pl.when(pl.program_id(0) == 0)
    def _():
        first = span_ref[0] == 0
        i = lax.broadcasted_iota(jnp.int32, (rows, near), 0)
        j = lax.broadcasted_iota(jnp.int32, (rows, near), 1)
        low = jnp.where(first, WINDOW, 0)
        ok = (j > i) & (j <= i + WINDOW) & (j >= low)
        bias_ref[:, :near] = jnp.where(ok, 0.0, NEG)
        for b in range(4):
            for level in range(LEVELS):
                for slot in range(2):
                    hit = (valid_ref[b, level] > 0) & (lists_ref[b, level] == used_ref[level, slot])
                    value = jnp.where(hit, 0.0, NEG)
                    at = near + (level * 2 + slot) * BLOCK
                    bias_ref[b * BLOCK:(b + 1) * BLOCK, at:at + BLOCK] = jnp.full(
                        (BLOCK, BLOCK), value, jnp.float32
                    )

    at = 0
    for ref, blocks in ((prev_ref, 4), (own_ref, 4), (far0_ref, 2), (far1_ref, 2), (far2_ref, 2)):
        for b in range(blocks):
            k_ref[at:at + BLOCK, :] = ref[b, 0]
            v_ref[at:at + BLOCK, :] = ref[b, 1]
            at += BLOCK
    q = qd_ref[:, 0].reshape(rows, HEAD_DIM)
    d = qd_ref[:, 1].reshape(rows, HEAD_DIM)
    s = dot_nt(q, k_ref[...]) * scale + bias_ref[...]
    m = jnp.max(s, -1, keepdims=True)
    p = jnp.exp(s - m)
    total = jnp.sum(p, -1, keepdims=True)
    w = p * (1.0 / total)
    wb = w.astype(jnp.bfloat16)
    att = dot_nn(wb, v_ref[...]).astype(jnp.bfloat16)
    att_ref[...] = att.reshape(4, BLOCK, HEAD_DIM)
    delta = jnp.sum(d.astype(jnp.float32) * att.astype(jnp.float32), -1, keepdims=True)
    dp = dot_nt(d, v_ref[...])
    ds = (w * (dp - delta)).astype(jnp.bfloat16)
    gq_ref[...] = (dot_nn(ds, k_ref[...]) * scale).astype(jnp.bfloat16)
    gk = dot_tn(ds, q) * scale
    gv = dot_tn(wb, d)
    gown_ref[0] = gk[WINDOW:near]
    gown_ref[1] = gv[WINDOW:near]
    gprev_ref[:, 0] = gk[:WINDOW].astype(jnp.bfloat16).reshape(4, BLOCK, HEAD_DIM)
    gprev_ref[:, 1] = gv[:WINDOW].astype(jnp.bfloat16).reshape(4, BLOCK, HEAD_DIM)
    for level, ref in enumerate((gfar0_ref, gfar1_ref, gfar2_ref)):
        a = near + level * 2 * BLOCK
        ref[:, 0] = gk[a:a + 2 * BLOCK].astype(jnp.bfloat16).reshape(2, BLOCK, HEAD_DIM)
        ref[:, 1] = gv[a:a + 2 * BLOCK].astype(jnp.bfloat16).reshape(2, BLOCK, HEAD_DIM)


def attend(span, lists, valid, used, qd, own, prev, fars):
    cols = qd.shape[-1]
    heads = cols // HEAD_DIM
    rows = 4 * BLOCK
    keys = WINDOW + rows + 2 * LEVELS * BLOCK

    def piece(*lead):
        return pl.BlockSpec(lead + (HEAD_DIM,), lambda h, *_: (0,) * len(lead) + (h,))

    four, two = piece(4, 2, BLOCK), piece(2, 2, BLOCK)
    bf = jnp.bfloat16
    return pl.pallas_call(
        attend_body,
        out_shape=[
            jax.ShapeDtypeStruct((4, BLOCK, cols), bf),
            jax.ShapeDtypeStruct((rows, cols), bf),
            jax.ShapeDtypeStruct((2, rows, cols), jnp.float32),
            jax.ShapeDtypeStruct((4, 2, BLOCK, cols), bf),
        ] + [jax.ShapeDtypeStruct((2, 2, BLOCK, cols), bf)] * LEVELS,
        grid_spec=pltpu.PrefetchScalarGridSpec(
            num_scalar_prefetch=4,
            grid=(heads,),
            in_specs=[four, four, four, two, two, two],
            out_specs=[piece(4, BLOCK), piece(rows), piece(2, rows), four, two, two, two],
            scratch_shapes=[
                pltpu.VMEM((rows, keys), jnp.float32),
                pltpu.VMEM((keys, HEAD_DIM), bf),
                pltpu.VMEM((keys, HEAD_DIM), bf),
            ],
        ),
        name="attend",
    )(span, lists, valid, used, qd, own, prev, *fars)


def total_body(idx_ref, gown_ref, gprev_ref, gfar0_ref, gfar1_ref, gfar2_ref, gk_ref, gv_ref, acc_ref):
    for b in range(4):
        for which in range(2):
            acc_ref[b, which] = gown_ref[which, b * BLOCK:(b + 1) * BLOCK] + gprev_ref[b, which].astype(jnp.float32)
    for level, ref in enumerate((gfar0_ref, gfar1_ref, gfar2_ref)):
        for slot in range(2):
            at = idx_ref[level, slot]
            acc_ref[at] += ref[slot].astype(jnp.float32)
    for b in range(4):
        gk_ref[b * BLOCK:(b + 1) * BLOCK, :] = acc_ref[b, 0].astype(jnp.bfloat16)
        gv_ref[b * BLOCK:(b + 1) * BLOCK, :] = acc_ref[b, 1].astype(jnp.bfloat16)


def total(idx, gown, gprev, gfars):
    cols = gown.shape[-1]
    rows = 4 * BLOCK
    step = 256

    def piece(*lead):
        return pl.BlockSpec(lead + (step,), lambda h, *_: (0,) * len(lead) + (h,))

    out = jax.ShapeDtypeStruct((rows, cols), jnp.bfloat16)
    return pl.pallas_call(
        total_body,
        out_shape=[out, out],
        grid_spec=pltpu.PrefetchScalarGridSpec(
            num_scalar_prefetch=1,
            grid=(cols // step,),
            in_specs=[piece(2, rows), piece(4, 2, BLOCK)] + [piece(2, 2, BLOCK)] * LEVELS,
            out_specs=[piece(rows), piece(rows)],
            scratch_shapes=[pltpu.VMEM((4, 2, BLOCK, step), jnp.float32)],
        ),
        name="total",
    )(idx, gown, gprev, *gfars)


def spread(x):
    return lax.all_to_all(x, "head", split_axis=0, concat_axis=0)


def per_device(q_tokens, k_tokens, v_tokens, grad_out, block_lists, block_valid):
    parts = lax.axis_size("head")
    span = lax.axis_index("seq").astype(jnp.int32).reshape(1)
    used = jnp.stack([jnp.min(block_lists, 0), jnp.max(block_lists, 0)], 1)
    asked = jnp.stack([passed_along(used[level], -2 * 4**level) for level in range(LEVELS)])
    own = spread(pack_pair(k_tokens, v_tokens, parts))
    picked = pick_blocks(asked, own)
    fars = [None] * LEVELS
    for level in reversed(range(LEVELS)):
        fars[level] = passed_along(picked[level], 2 * 4**level)
    prev = passed_along(own, 1)
    qd = spread(pack_pair(q_tokens, grad_out, parts))
    att, grad_q, gown, gprev, *gfars = attend(
        span, block_lists, block_valid, used, qd, own, prev, fars
    )
    back = [None] * LEVELS
    for level in reversed(range(LEVELS)):
        back[level] = passed_along(gfars[level], -2 * 4**level)
    back_prev = passed_along(gprev, -1)
    attended = spread(att).transpose(1, 0, 2).reshape(q_tokens.shape)
    grad_k, grad_v = total(asked, gown, back_prev, back)
    return attended, grad_q, grad_k, grad_v


def solution(mesh):
    tokens = P(("seq", "head"), None)
    return jax.shard_map(
        per_device,
        mesh=mesh,
        in_specs=(tokens,) * 4 + (P("seq", None),) * 2,
        out_specs=(tokens,) + (P("seq", "head"),) * 3,
        check_vma=False,
    )
```

time: 679 us -> 275 us (0.41)
  waiting for transfers between devices: 380 us -> 199 us
  starting transfers between devices: 147 us -> 41.6 us
  local copies, waits for them, and re-layouts: 83.9 us -> 3.17 us
  matrix products: 46.5 us -> 0 us
  Pallas kernels: 0 us -> 28.6 us
  other arithmetic: 14.5 us -> 0.7 us
    ppermute x16 -> x11, waiting for transfers between devices: 363 us -> 187 us  [passed_along(): return lax.ppermute(shard, 'seq', pairs)]
    ppermute x16 -> x11, starting transfers between devices: 121 us -> 27.7 us  [passed_along(): return lax.ppermute(shard, 'seq', pairs)]
    dot_general x18 -> x0, matrix products: 46.5 us -> none  [the longest x3 9.97 us: per_device(): jnp.einsum('bs,btc->stc', spread, value_grad_far[:, position], precision=...]
    pallas_call x0 -> x5, Pallas kernels: none -> 28.6 us  [the longest x1 13.7 us: attend(): pl.pallas_call(attend_body, out_shape=[jax.ShapeDtypeStruct((4, BLOCK, co...]
    reshape x10 -> x1, local copies, waits for them, and re-layouts: 21.4 us -> 0.83 us  [per_device(): attended = spread(att).transpose(1, 0, 2).reshape(q_tokens.shape)]
    all_to_all x5 -> x3, starting transfers between devices: 26.3 us -> 13.9 us  [spread(): return lax.all_to_all(x, 'head', split_axis=0, concat_axis=0)]
    gather x6 -> x0, local copies, waits for them, and re-layouts: 11.9 us -> none  [the longest x3 6.45 us: per_device(): jnp.take(far_keys[reach_level], slot_rows[reach_level], axis=0)]
    dot_general x7 -> x0, local copies, waits for them, and re-layouts: 11.1 us -> none  [the longest x3 6.26 us: per_device(): jnp.einsum('bs,btc->stc', spread, value_grad_far[:, position], precision=...]
  transfers between devices with their start and end apart: 21 -> 14, of which waited for: 6 -> 8; matrix products, arithmetic and copies ran while one was open for 12% -> 1% of each run, Pallas kernels for 0% -> 2%
where the time goes in v1:
time: 275 us; the launch traced here: 274 us
  waiting for transfers between devices  199 us (72%)
  starting transfers between devices  41.6 us (15%)
  Pallas kernels  28.6 us (10%)
  local copies, waits for them, and re-layouts  3.17 us (1%)
    ppermute x11, waiting for transfers between devices, passed_along(): return lax.ppermute(shard, 'seq', pairs)  187 us
    ppermute x11, starting transfers between devices, passed_along(): return lax.ppermute(shard, 'seq', pairs)  27.7 us
    all_to_all x3, starting transfers between devices, spread(): return lax.all_to_all(x, 'head', split_axis=0, concat_axis=0)  13.9 us
    pallas_call x1, Pallas kernels, attend(): pl.pallas_call(attend_body, out_shape=[jax.ShapeDtypeStruct((4, BLOCK, co...  13.7 us
    all_to_all x3, waiting for transfers between devices, spread(): return lax.all_to_all(x, 'head', split_axis=0, concat_axis=0)  12.5 us
    pallas_call x2, Pallas kernels, pack_pair(): pl.pallas_call(pack_body, out_shape=jax.ShapeDtypeStruct((parts, 2, rows,...  6.82 us
  transfers between devices with their start and end apart: 14, of which 8 were waited for; matrix products, arithmetic and copies ran while one was open for 1% of the time, Pallas kernels for 2%

profile of v1, /device:TPU:32, one launch (start us, length us, event | category | flops | bytes accessed | tf_op | source)
XLA Modules:
  0.0 274.1 jit_solution(8909528718324388386)
XLA Ops:
  0.6 3.4 %pack_pair.3 = bf16[4,2,64,1024]{3,2,1,0:T(8,128)(2,1)} custom-call(bf16[64,4096]{1,0:T(8,128)(2,1)} %a_ref.3, bf16[64,4096]{1,0:T(8,128)(2,1)} %b_ref.3), custom_call_target="tpu_custom_call" | custom-call | tf_op jit(solution)/shard_map/pack_pair/pallas_call | solution.py:29
  4.0 5.3 %all-to-all-start.1 = ((bf16[4,2,64,1024]{3,2,1,0:T(8,128)(2,1)}), bf16[4,2,64,1024]{3,2,1,0:T(8,128)(2,1)S(1)}, u32[]{:S(2)}, u32[]{:S(2)}) async-start(bf16[4,2,64,1024]{3,2,1,0:T(8,128)(2,1)} %pack_pair.3), calls=%async_computation.1 | async-start | bytes 2097152 | tf_op jit(solution)/shard_map/all_to_all | solution.py:214
  9.3 0.0 copy-start.8
  9.3 3.4 %pack_pair.2 = bf16[4,2,64,1024]{3,2,1,0:T(8,128)(2,1)} custom-call(bf16[64,4096]{1,0:T(8,128)(2,1)} %a_ref.2, bf16[64,4096]{1,0:T(8,128)(2,1)} %b_ref.2), custom_call_target="tpu_custom_call" | custom-call | tf_op jit(solution)/shard_map/pack_pair/pallas_call | solution.py:29
  12.8 9.4 %all-to-all-done.1.kv_ref.own_ref = bf16[4,2,64,1024]{3,2,1,0:T(8,128)(2,1)S(1)} async-done(((bf16[4,2,64,1024]{3,2,1,0:T(8,128)(2,1)}), bf16[4,2,64,1024]{3,2,1,0:T(8,128)(2,1)S(1)}, u32[]{:S(2)}, u32[]{:S(2)}) %all-to-all-start.1) | async-done | bytes 1048608 | tf_op jit(solution)/shard_map/all_to_all | solution.py:214
  22.1 5.1 %all-to-all-start = ((bf16[4,2,64,1024]{3,2,1,0:T(8,128)(2,1)}), bf16[4,2,64,1024]{3,2,1,0:T(8,128)(2,1)S(1)}, u32[]{:S(2)}, u32[]{:S(2)}) async-start(bf16[4,2,64,1024]{3,2,1,0:T(8,128)(2,1)} %pack_pair.2), calls=%async_computation | async-start | bytes 2097152 | tf_op jit(solution)/shard_map/all_to_all | solution.py:214
  27.3 1.8 collective-permute-start
  29.1 0.0 copy-done.8
  29.1 0.1 copy.13
  29.2 0.1 copy.12
  29.3 0.1 pad_add_fusion.used_ref
  29.4 1.3 collective-permute-start.1
  30.7 1.3 collective-permute-start.3
  32.0 1.3 collective-permute-start.2
  33.3 21.8 %collective-permute-done.1 = s32[2]{0:T(128)S(1)} collective-permute-done((s32[2]{0:T(128)S(1)}, s32[2]{0:T(128)S(1)}, u32[]{:S(2)}, u32[]{:S(2)}) %collective-permute-start.1) | collective-permute-done | bytes 40 | tf_op jit(solution)/shard_map/ppermute | solution.py:18
  55.1 0.0 collective-permute-done.3
  55.1 0.0 collective-permute-done.2
  55.1 0.6 pad_add_fusion.1.idx_ref
  55.7 0.0 copy-done
  55.7 3.1 %pick_blocks.1 = (bf16[2,2,64,1024]{3,2,1,0:T(8,128)(2,1)}, bf16[2,2,64,1024]{3,2,1,0:T(8,128)(2,1)}, bf16[2,2,64,1024]{3,2,1,0:T(8,128)(2,1)}) custom-call(s32[3,2]{1,0:T(4,128)} %pad_add_fusion.1.idx_ref, bf16[4,2,64,1024]{3,2,1,0:T(8,128)(2,1)} %copy-done), custom_call_target="tpu_custom_call" | custom-call | tf_op jit(solution)/shard_map/pick_blocks/pallas_call | solution.py:57
  58.8 2.3 collective-permute-start.4
  61.1 5.4 %collective-permute-start.5 = (bf16[2,2,64,1024]{3,2,1,0:T(8,128)(2,1)}, bf16[2,2,64,1024]{3,2,1,0:T(8,128)(2,1)}, u32[]{:S(2)}, u32[]{:S(2)}) collective-permute-start(bf16[2,2,64,1024]{3,2,1,0:T(8,128)(2,1)} %get-tuple-element.17), channel_id=1, source_target_pairs={{0,32},{4,36},{8,40},{12,44},{16,48},{20,52},{24,56},{28,60},{32,6... | collective-permute-start | bytes 1572872 | tf_op jit(solution)/shard_map/ppermute | solution.py:18
  66.4 9.2 %collective-permute-start.6 = (bf16[2,2,64,1024]{3,2,1,0:T(8,128)(2,1)}, bf16[2,2,64,1024]{3,2,1,0:T(8,128)(2,1)}, u32[]{:S(2)}, u32[]{:S(2)}) collective-permute-start(bf16[2,2,64,1024]{3,2,1,0:T(8,128)(2,1)} %get-tuple-element.18), channel_id=1, source_target_pairs={{0,128},{4,132},{8,136},{12,140},{16,144},{20,148},{24,152},{28,15... | collective-permute-start | bytes 1572872 | tf_op jit(solution)/shard_map/ppermute | solution.py:18
  75.6 0.0 all-to-all-done.qd_ref
  75.6 0.0 collective-permute-done.4.far0_ref
  75.6 0.9 collective-permute-done.5.far1_ref
  76.6 20.1 %collective-permute-done.6.far2_ref = bf16[2,2,64,1024]{3,2,1,0:T(8,128)(2,1)} collective-permute-done((bf16[2,2,64,1024]{3,2,1,0:T(8,128)(2,1)}, bf16[2,2,64,1024]{3,2,1,0:T(8,128)(2,1)}, u32[]{:S(2)}, u32[]{:S(2)}) %collective-permute-start.6) | collective-permute-done | bytes 524320 | tf_op jit(solution)/shard_map/ppermute | solution.py:18
  96.6 0.0 collective-permute-done.prev_ref
  96.6 0.0 copy-done.7
  96.6 0.0 copy-done.1
  96.6 1.0 copy-done.2
  97.6 13.7 %attend.1 = (bf16[4,64,1024]{2,1,0:T(8,128)(2,1)}, bf16[256,1024]{1,0:T(8,128)(2,1)}, f32[2,256,1024]{2,1,0:T(8,128)}, bf16[4,2,64,1024]{3,2,1,0:T(8,128)(2,1)},...) custom-call(s32[1]{0:T(128)} %bitcast.span_ref, ...), custom_call_target="tpu_custom_call" | custom-call | tf_op jit(solution)/shard_map/attend/pallas_call | solution.py:154
  111.3 1.3 collective-permute-start.7
  112.6 3.5 %all-to-all-start.2 = ((bf16[4,64,1024]{2,1,0:T(8,128)(2,1)}), bf16[4,64,1024]{2,1,0:T(8,128)(2,1)S(1)}, u32[]{:S(2)}, u32[]{:S(2)}) async-start(bf16[4,64,1024]{2,1,0:T(8,128)(2,1)} %get-tuple-element.19), calls=%async_computation.2 | async-start | bytes 1048576 | tf_op jit(solution)/shard_map/all_to_all | solution.py:214
  116.1 1.3 collective-permute-start.8
  117.4 1.3 collective-permute-start.9
  118.7 1.3 collective-permute-start.10
  120.0 3.1 %all-to-all-done.2 = bf16[4,64,1024]{2,1,0:T(8,128)(2,1)S(1)} async-done(((bf16[4,64,1024]{2,1,0:T(8,128)(2,1)}), bf16[4,64,1024]{2,1,0:T(8,128)(2,1)S(1)}, u32[]{:S(2)}, u32[]{:S(2)}) %all-to-all-start.2) | async-done | bytes 524320 | tf_op jit(solution)/shard_map/all_to_all | solution.py:214
  123.1 0.8 copy.15
  124.0 10.8 %collective-permute-done.8.gfar0_ref = bf16[2,2,64,1024]{3,2,1,0:T(8,128)(2,1)S(1)} collective-permute-done((bf16[2,2,64,1024]{3,2,1,0:T(8,128)(2,1)}, bf16[2,2,64,1024]{3,2,1,0:T(8,128)(2,1)S(1)}, u32[]{:S(2)}, u32[]{:S(2)}) %collective-permute-start.8) | collective-permute-done | bytes 524320 | tf_op jit(solution)/shard_map/ppermute | solution.py:18
  134.7 45.9 %collective-permute-done.9.gfar1_ref = bf16[2,2,64,1024]{3,2,1,0:T(8,128)(2,1)S(1)} collective-permute-done((bf16[2,2,64,1024]{3,2,1,0:T(8,128)(2,1)}, bf16[2,2,64,1024]{3,2,1,0:T(8,128)(2,1)S(1)}, u32[]{:S(2)}, u32[]{:S(2)}) %collective-permute-start.9) | collective-permute-done | bytes 524320 | tf_op jit(solution)/shard_map/ppermute | solution.py:18
  180.7 87.3 %collective-permute-done.10.gfar2_ref = bf16[2,2,64,1024]{3,2,1,0:T(8,128)(2,1)S(1)} collective-permute-done((bf16[2,2,64,1024]{3,2,1,0:T(8,128)(2,1)}, bf16[2,2,64,1024]{3,2,1,0:T(8,128)(2,1)S(1)}, u32[]{:S(2)}, u32[]{:S(2)}) %collective-permute-start.10) | collective-permute-done | bytes 524320 | tf_op jit(solution)/shard_map/ppermute | solution.py:18
  268.0 0.0 collective-permute-done.7.gprev_ref
  268.0 0.0 copy-done.4
  268.0 0.0 copy-done.5
  268.0 0.8 copy-done.6
  268.8 0.4 copy-done.3
  269.1 4.9 %total.1 = (bf16[256,1024]{1,0:T(8,128)(2,1)}, bf16[256,1024]{1,0:T(8,128)(2,1)}) custom-call(s32[3,2]{1,0:T(4,128)} %pad_add_fusion.1.idx_ref, f32[2,256,1024]{2,1,0:T(8,128)} %get-tuple-element.21.gown_ref, bf16[4,2,64,1024]{3,2,1,0:T(8,128)(2,1)} %copy-done.3, bf16[2,2,64,1024]{3,2,1,0:T(8,128)(2,1)} %copy-done.4, bf16[2,2,64,1024]{3,2,1,0:T(8,128)(2,1)} %copy-done.5, ...), custom_call_target="tpu_custom_call" | custom-call | tf_op jit(solution)/shard_map/total/pallas_call | solution.py:199
  (10 shorter events, 0.0 us)
Async XLA Ops:
  4.0 18.1 %all-to-all-start.1 = ((bf16[4,2,64,1024]{3,2,1,0:T(8,128)(2,1)}), bf16[4,2,64,1024]{3,2,1,0:T(8,128)(2,1)S(1)}, u32[]{:S(2)}, u32[]{:S(2)}) async-start(bf16[4,2,64,1024]{3,2,1,0:T(8,128)(2,1)} %pack_pair.3), calls=%async_computation.1 | async-start | bytes 2097152 | tf_op jit(solution)/shard_map/all_to_all | solution.py:214
  9.3 19.8 %copy-start.8 = (s32[4,3]{1,0:T(4,128)S(1)}, s32[4,3]{1,0:T(4,128)}, u32[]{:S(2)}) copy-start(s32[4,3]{1,0:T(4,128)} %lists_ref.1) | copy-start | bytes 148
  22.1 33.6 %copy-start = (bf16[4,2,64,1024]{3,2,1,0:T(8,128)(2,1)}, bf16[4,2,64,1024]{3,2,1,0:T(8,128)(2,1)S(1)}, u32[]{:S(2)}) copy-start(bf16[4,2,64,1024]{3,2,1,0:T(8,128)(2,1)S(1)} %all-to-all-done.1.kv_ref.own_ref) | copy-start | bytes 3145732
  22.1 53.5 %all-to-all-start = ((bf16[4,2,64,1024]{3,2,1,0:T(8,128)(2,1)}), bf16[4,2,64,1024]{3,2,1,0:T(8,128)(2,1)S(1)}, u32[]{:S(2)}, u32[]{:S(2)}) async-start(bf16[4,2,64,1024]{3,2,1,0:T(8,128)(2,1)} %pack_pair.2), calls=%async_computation | async-start | bytes 2097152 | tf_op jit(solution)/shard_map/all_to_all | solution.py:214
  27.3 69.4 %collective-permute-start = (bf16[4,2,64,1024]{3,2,1,0:T(8,128)(2,1)S(1)}, bf16[4,2,64,1024]{3,2,1,0:T(8,128)(2,1)S(1)}, u32[]{:S(2)}, u32[]{:S(2)}) collective-permute-start(bf16[4,2,64,1024]{3,2,1,0:T(8,128)(2,1)S(1)} %all-to-all-done.1.kv_ref.own_ref), channel_id=1, source_target_pairs={{0,4},{4,8},{8,12},{12,16},{16,20},{20,24},{24,28},{28,32},{32,36}... | collective-permute-start | bytes 3145736 | tf_op jit(solution)/shard_map/ppermute | solution.py:18
  29.4 67.2 %copy-start.7 = (s32[3,2]{1,0:T(4,128)}, s32[3,2]{1,0:T(4,128)S(1)}, u32[]{:S(2)}) copy-start(s32[3,2]{1,0:T(4,128)S(1)} %pad_add_fusion.used_ref) | copy-start | bytes 76
  29.4 25.7 %collective-permute-start.1 = (s32[2]{0:T(128)S(1)}, s32[2]{0:T(128)S(1)}, u32[]{:S(2)}, u32[]{:S(2)}) collective-permute-start(s32[2]{0:T(128)S(1)} %get-tuple-element.30), channel_id=1, source_target_pairs={{8,0},{12,4},{16,8},{20,12},{24,16},{28,20},{32,24},{36,28},{40,32... | collective-permute-start | bytes 32 | tf_op jit(solution)/shard_map/ppermute | solution.py:18
  30.7 24.4 %collective-permute-start.3 = (s32[2]{0:T(128)S(1)}, s32[2]{0:T(128)S(1)}, u32[]{:S(2)}, u32[]{:S(2)}) collective-permute-start(s32[2]{0:T(128)S(1)} %get-tuple-element.31), channel_id=1, source_target_pairs={{128,0},{132,4},{136,8},{140,12},{144,16},{148,20},{152,24},{156,2... | collective-permute-start | bytes 32 | tf_op jit(solution)/shard_map/ppermute | solution.py:18
  32.0 23.1 %collective-permute-start.2 = (s32[2]{0:T(128)S(1)}, s32[2]{0:T(128)S(1)}, u32[]{:S(2)}, u32[]{:S(2)}) collective-permute-start(s32[2]{0:T(128)S(1)} %get-tuple-element.32), channel_id=1, source_target_pairs={{32,0},{36,4},{40,8},{44,12},{48,16},{52,20},{56,24},{60,28},{64,3... | collective-permute-start | bytes 32 | tf_op jit(solution)/shard_map/ppermute | solution.py:18
  58.8 16.8 %collective-permute-start.4 = (bf16[2,2,64,1024]{3,2,1,0:T(8,128)(2,1)}, bf16[2,2,64,1024]{3,2,1,0:T(8,128)(2,1)}, u32[]{:S(2)}, u32[]{:S(2)}) collective-permute-start(bf16[2,2,64,1024]{3,2,1,0:T(8,128)(2,1)} %get-tuple-element.16), channel_id=1, source_target_pairs={{0,8},{4,12},{8,16},{12,20},{16,24},{20,28},{24,32},{28,36},{32,40... | collective-permute-start | bytes 1572872 | tf_op jit(solution)/shard_map/ppermute | solution.py:18
  61.1 15.5 %collective-permute-start.5 = (bf16[2,2,64,1024]{3,2,1,0:T(8,128)(2,1)}, bf16[2,2,64,1024]{3,2,1,0:T(8,128)(2,1)}, u32[]{:S(2)}, u32[]{:S(2)}) collective-permute-start(bf16[2,2,64,1024]{3,2,1,0:T(8,128)(2,1)} %get-tuple-element.17), channel_id=1, source_target_pairs={{0,32},{4,36},{8,40},{12,44},{16,48},{20,52},{24,56},{28,60},{32,6... | collective-permute-start | bytes 1572872 | tf_op jit(solution)/shard_map/ppermute | solution.py:18
  66.4 30.2 %collective-permute-start.6 = (bf16[2,2,64,1024]{3,2,1,0:T(8,128)(2,1)}, bf16[2,2,64,1024]{3,2,1,0:T(8,128)(2,1)}, u32[]{:S(2)}, u32[]{:S(2)}) collective-permute-start(bf16[2,2,64,1024]{3,2,1,0:T(8,128)(2,1)} %get-tuple-element.18), channel_id=1, source_target_pairs={{0,128},{4,132},{8,136},{12,140},{16,144},{20,148},{24,152},{28,15... | collective-permute-start | bytes 1572872 | tf_op jit(solution)/shard_map/ppermute | solution.py:18
  75.6 21.0 %copy-start.1 = (bf16[4,2,64,1024]{3,2,1,0:T(8,128)(2,1)}, bf16[4,2,64,1024]{3,2,1,0:T(8,128)(2,1)S(1)}, u32[]{:S(2)}) copy-start(bf16[4,2,64,1024]{3,2,1,0:T(8,128)(2,1)S(1)} %all-to-all-done.qd_ref) | copy-start | bytes 3145732
  96.6 1.0 copy-start.2
  111.3 156.6 %collective-permute-start.7 = (bf16[4,2,64,1024]{3,2,1,0:T(8,128)(2,1)}, bf16[4,2,64,1024]{3,2,1,0:T(8,128)(2,1)S(1)}, u32[]{:S(2)}, u32[]{:S(2)}) collective-permute-start(bf16[4,2,64,1024]{3,2,1,0:T(8,128)(2,1)} %get-tuple-element.22), channel_id=1, source_target_pairs={{4,0},{8,4},{12,8},{16,12},{20,16},{24,20},{28,24},{32,28},{36,32}... | collective-permute-start | bytes 3145736 | tf_op jit(solution)/shard_map/ppermute | solution.py:18
  112.6 10.5 %all-to-all-start.2 = ((bf16[4,64,1024]{2,1,0:T(8,128)(2,1)}), bf16[4,64,1024]{2,1,0:T(8,128)(2,1)S(1)}, u32[]{:S(2)}, u32[]{:S(2)}) async-start(bf16[4,64,1024]{2,1,0:T(8,128)(2,1)} %get-tuple-element.19), calls=%async_computation.2 | async-start | bytes 1048576 | tf_op jit(solution)/shard_map/all_to_all | solution.py:214
  116.1 18.6 %collective-permute-start.8 = (bf16[2,2,64,1024]{3,2,1,0:T(8,128)(2,1)}, bf16[2,2,64,1024]{3,2,1,0:T(8,128)(2,1)S(1)}, u32[]{:S(2)}, u32[]{:S(2)}) collective-permute-start(bf16[2,2,64,1024]{3,2,1,0:T(8,128)(2,1)} %get-tuple-element.23), channel_id=1, source_target_pairs={{8,0},{12,4},{16,8},{20,12},{24,16},{28,20},{32,24},{36,28},{40,32... | collective-permute-start | bytes 1572872 | tf_op jit(solution)/shard_map/ppermute | solution.py:18
  117.4 63.3 %collective-permute-start.9 = (bf16[2,2,64,1024]{3,2,1,0:T(8,128)(2,1)}, bf16[2,2,64,1024]{3,2,1,0:T(8,128)(2,1)S(1)}, u32[]{:S(2)}, u32[]{:S(2)}) collective-permute-start(bf16[2,2,64,1024]{3,2,1,0:T(8,128)(2,1)} %get-tuple-element.24), channel_id=1, source_target_pairs={{32,0},{36,4},{40,8},{44,12},{48,16},{52,20},{56,24},{60,28},{64,3... | collective-permute-start | bytes 1572872 | tf_op jit(solution)/shard_map/ppermute | solution.py:18
  118.7 149.3 %collective-permute-start.10 = (bf16[2,2,64,1024]{3,2,1,0:T(8,128)(2,1)}, bf16[2,2,64,1024]{3,2,1,0:T(8,128)(2,1)S(1)}, u32[]{:S(2)}, u32[]{:S(2)}) collective-permute-start(bf16[2,2,64,1024]{3,2,1,0:T(8,128)(2,1)} %get-tuple-element.25), channel_id=1, source_target_pairs={{128,0},{132,4},{136,8},{140,12},{144,16},{148,20},{152,24},{156,2... | collective-permute-start | bytes 1572872 | tf_op jit(solution)/shard_map/ppermute | solution.py:18
  134.7 133.2 %copy-start.4 = (bf16[2,2,64,1024]{3,2,1,0:T(8,128)(2,1)}, bf16[2,2,64,1024]{3,2,1,0:T(8,128)(2,1)S(1)}, u32[]{:S(2)}) copy-start(bf16[2,2,64,1024]{3,2,1,0:T(8,128)(2,1)S(1)} %collective-permute-done.8.gfar0_ref) | copy-start | bytes 1572868
  180.7 87.3 %copy-start.5 = (bf16[2,2,64,1024]{3,2,1,0:T(8,128)(2,1)}, bf16[2,2,64,1024]{3,2,1,0:T(8,128)(2,1)S(1)}, u32[]{:S(2)}) copy-start(bf16[2,2,64,1024]{3,2,1,0:T(8,128)(2,1)S(1)} %collective-permute-done.9.gfar1_ref) | copy-start | bytes 1572868
  268.0 0.8 copy-start.6
  268.0 1.1 copy-start.3

commit v2 on v1

--- a/solution.py
+++ b/solution.py
@@ -1,3 +1,5 @@
+import functools
+
 import jax
 import jax.numpy as jnp
 from jax import lax
@@ -12,10 +14,51 @@
 NEG = -1e30
 
 
-def passed_along(shard, by):
+DETOURS = {1: {15: 0}, 2: {15: 1}, 8: {14: 6, 15: 7}}
+PLANE = 16
+
+
+def pairs_of(peers, by, detour):
+    pairs = []
+    for i in range(peers):
+        if i + by < peers:
+            to = i + by
+            if detour and to // PLANE > i // PLANE:
+                at = DETOURS[by].get(i % PLANE)
+                to = to if at is None else i // PLANE * PLANE + at
+            pairs.append((i, to))
+    return pairs
+
+
+def passed(shard, by, detour=False):
     peers = lax.axis_size("seq")
-    pairs = [(i, i + by) for i in range(peers) if 0 <= i + by < peers]
+    pairs = pairs_of(peers, abs(by), detour)
+    if by < 0:
+        pairs = [(peers - 1 - i, peers - 1 - j) for i, j in pairs]
     return lax.ppermute(shard, "seq", pairs)
+
+
+def stepped(shard, sign):
+    peers = lax.axis_size("seq")
+    relays = [at for table in DETOURS.values() for at in table.values()]
+    pairs = [(i, i + PLANE) for i in range(peers - PLANE) if i % PLANE in relays]
+    if sign < 0:
+        pairs = [(peers - 1 - i, peers - 1 - j) for i, j in pairs]
+    return lax.ppermute(shard, "seq", pairs)
+
+
+def relayed(first, second, third, sign):
+    peers = lax.axis_size("seq")
+    at = lax.axis_index("seq")
+    at = at if sign > 0 else peers - 1 - at
+    here = at % PLANE
+    hits = [
+        functools.reduce(jnp.logical_or, [here == v for v in DETOURS[by].values()]) for by in (1, 2, 8)
+    ]
+    outgoing = jnp.where(hits[0], first, jnp.where(hits[1], second, third))
+    extra = stepped(outgoing, sign)
+    got = jnp.where(at >= PLANE, 1, 2)
+    return extra, jnp.stack([jnp.where(hit, got, 0) for hit in hits]).astype(jnp.int32)
 
 
 def pack_body(a_ref, b_ref, out_ref):
@@ -39,13 +82,12 @@
 def pick_body(idx_ref, kv_ref, *rest):
     outs, sems = rest[:-1], rest[-1]
     copies = []
-    for level in reversed(range(LEVELS)):
+    for level in range(LEVELS):
         for slot in range(2):
-            copies.append(
-                pltpu.make_async_copy(
-                    kv_ref.at[idx_ref[level, slot]], outs[level].at[slot], sems.at[level, slot]
-                )
-            )
+            copies.append((kv_ref.at[idx_ref[level, slot]], outs[level].at[slot]))
+    copies.append((kv_ref.at[:2], outs[LEVELS]))
+    copies.append((kv_ref.at[2:], outs[LEVELS + 1]))
+    copies = [pltpu.make_async_copy(src, dst, sems.at[n]) for n, (src, dst) in enumerate(copies)]
     for copy in copies:
         copy.start()
     for copy in copies:
@@ -56,13 +98,13 @@
     shape = jax.ShapeDtypeStruct((2,) + kv.shape[1:], kv.dtype)
     return pl.pallas_call(
         pick_body,
-        out_shape=[shape] * LEVELS,
+        out_shape=[shape] * (LEVELS + 2),
         grid_spec=pltpu.PrefetchScalarGridSpec(
             num_scalar_prefetch=1,
             in_specs=[pl.BlockSpec(memory_space=pltpu.VMEM)],
-            out_specs=[pl.BlockSpec(memory_space=pl.ANY)] * LEVELS,
+            out_specs=[pl.BlockSpec(memory_space=pl.ANY)] * (LEVELS + 2),
             grid=(1,),
-            scratch_shapes=[pltpu.SemaphoreType.DMA((LEVELS, 2))],
+            scratch_shapes=[pltpu.SemaphoreType.DMA((2 * LEVELS + 2,))],
         ),
         name="pick_blocks",
     )(idx, kv)
@@ -81,9 +123,9 @@
 
 
 def attend_body(
-    span_ref, lists_ref, valid_ref, used_ref,
-    qd_ref, own_ref, prev_ref, far0_ref, far1_ref, far2_ref,
-    att_ref, gq_ref, gown_ref, gprev_ref, gfar0_ref, gfar1_ref, gfar2_ref,
+    span_ref, lists_ref, valid_ref, used_ref, from_ref,
+    qd_ref, own_ref, prev0_ref, prev1_ref, far0_ref, far1_ref, far2_ref, extra_ref,
+    att_ref, gq_ref, gown_ref, gprev0_ref, gprev1_ref, gfar0_ref, gfar1_ref, gfar2_ref,
     bias_ref, k_ref, v_ref,
 ):
     rows = 4 * BLOCK
@@ -109,10 +151,16 @@
                     )
 
     at = 0
-    for ref, blocks in ((prev_ref, 4), (own_ref, 4), (far0_ref, 2), (far1_ref, 2), (far2_ref, 2)):
+    for ref, blocks, source in (
+        (prev0_ref, 2, 0), (prev1_ref, 2, None), (own_ref, 4, None),
+        (far0_ref, 2, 1), (far1_ref, 2, 2), (far2_ref, 2, None),
+    ):
         for b in range(blocks):
-            k_ref[at:at + BLOCK, :] = ref[b, 0]
-            v_ref[at:at + BLOCK, :] = ref[b, 1]
+            for which, out in enumerate((k_ref, v_ref)):
+                block = ref[b, which]
+                if source is not None:
+                    block = jnp.where(from_ref[source] == 1, extra_ref[b, which], block)
+                out[at:at + BLOCK, :] = block
             at += BLOCK
     q = qd_ref[:, 0].reshape(rows, HEAD_DIM)
     d = qd_ref[:, 1].reshape(rows, HEAD_DIM)
@@ -132,15 +180,15 @@
     gv = dot_tn(wb, d)
     gown_ref[0] = gk[WINDOW:near]
     gown_ref[1] = gv[WINDOW:near]
-    gprev_ref[:, 0] = gk[:WINDOW].astype(jnp.bfloat16).reshape(4, BLOCK, HEAD_DIM)
-    gprev_ref[:, 1] = gv[:WINDOW].astype(jnp.bfloat16).reshape(4, BLOCK, HEAD_DIM)
-    for level, ref in enumerate((gfar0_ref, gfar1_ref, gfar2_ref)):
-        a = near + level * 2 * BLOCK
+    for a, ref in (
+        (0, gprev0_ref), (2 * BLOCK, gprev1_ref),
+        (near, gfar0_ref), (near + 2 * BLOCK, gfar1_ref), (near + 4 * BLOCK, gfar2_ref),
+    ):
         ref[:, 0] = gk[a:a + 2 * BLOCK].astype(jnp.bfloat16).reshape(2, BLOCK, HEAD_DIM)
         ref[:, 1] = gv[a:a + 2 * BLOCK].astype(jnp.bfloat16).reshape(2, BLOCK, HEAD_DIM)
 
 
-def attend(span, lists, valid, used, qd, own, prev, fars):
+def attend(span, lists, valid, used, source, qd, own, prevs, fars, extra):
     cols = qd.shape[-1]
     heads = cols // HEAD_DIM
     rows = 4 * BLOCK
@@ -157,13 +205,12 @@
             jax.ShapeDtypeStruct((4, BLOCK, cols), bf),
             jax.ShapeDtypeStruct((rows, cols), bf),
             jax.ShapeDtypeStruct((2, rows, cols), jnp.float32),
-            jax.ShapeDtypeStruct((4, 2, BLOCK, cols), bf),
-        ] + [jax.ShapeDtypeStruct((2, 2, BLOCK, cols), bf)] * LEVELS,
+        ] + [jax.ShapeDtypeStruct((2, 2, BLOCK, cols), bf)] * (LEVELS + 2),
         grid_spec=pltpu.PrefetchScalarGridSpec(
-            num_scalar_prefetch=4,
+            num_scalar_prefetch=5,
             grid=(heads,),
-            in_specs=[four, four, four, two, two, two],
-            out_specs=[piece(4, BLOCK), piece(rows), piece(2, rows), four, two, two, two],
+            in_specs=[four, four] + [two] * (LEVELS + 3),
+            out_specs=[piece(4, BLOCK), piece(rows), piece(2, rows)] + [two] * (LEVELS + 2),
             scratch_shapes=[
                 pltpu.VMEM((rows, keys), jnp.float32),
                 pltpu.VMEM((keys, HEAD_DIM), bf),
@@ -171,23 +218,34 @@
             ],
         ),
         name="attend",
-    )(span, lists, valid, used, qd, own, prev, *fars)
-
-
-def total_body(idx_ref, gown_ref, gprev_ref, gfar0_ref, gfar1_ref, gfar2_ref, gk_ref, gv_ref, acc_ref):
+    )(span, lists, valid, used, source, qd, own, *prevs, *fars, extra)
+
+
+def total_body(
+    idx_ref, from_ref, gown_ref, gprev0_ref, gprev1_ref, gfar0_ref, gfar1_ref, gfar2_ref, extra_ref,
+    gk_ref, gv_ref, acc_ref,
+):
+    def part(ref, slot, source):
+        block = ref[slot].astype(jnp.float32)
+        if source is not None:
+            other = extra_ref[slot].astype(jnp.float32)
+            own = from_ref[source]
+            block = jnp.where(own == 0, block, jnp.where(own == 1, other, 0.0))
+        return block
+
     for b in range(4):
-        for which in range(2):
-            acc_ref[b, which] = gown_ref[which, b * BLOCK:(b + 1) * BLOCK] + gprev_ref[b, which].astype(jnp.float32)
-    for level, ref in enumerate((gfar0_ref, gfar1_ref, gfar2_ref)):
+        rows = slice(b * BLOCK, (b + 1) * BLOCK)
+        acc_ref[b] = gown_ref[:, rows] + (part(gprev0_ref, b, 0) if b < 2 else part(gprev1_ref, b - 2, None))
+    for level, (ref, source) in enumerate(((gfar0_ref, 1), (gfar1_ref, 2), (gfar2_ref, None))):
         for slot in range(2):
             at = idx_ref[level, slot]
-            acc_ref[at] += ref[slot].astype(jnp.float32)
+            acc_ref[at] += part(ref, slot, source)
     for b in range(4):
         gk_ref[b * BLOCK:(b + 1) * BLOCK, :] = acc_ref[b, 0].astype(jnp.bfloat16)
         gv_ref[b * BLOCK:(b + 1) * BLOCK, :] = acc_ref[b, 1].astype(jnp.bfloat16)
 
 
-def total(idx, gown, gprev, gfars):
+def total(idx, source, gown, gprevs, gfars, extra):
     cols = gown.shape[-1]
     rows = 4 * BLOCK
     step = 256
@@ -200,14 +258,14 @@
         total_body,
         out_shape=[out, out],
         grid_spec=pltpu.PrefetchScalarGridSpec(
-            num_scalar_prefetch=1,
+            num_scalar_prefetch=2,
             grid=(cols // step,),
-            in_specs=[piece(2, rows), piece(4, 2, BLOCK)] + [piece(2, 2, BLOCK)] * LEVELS,
+            in_specs=[piece(2, rows)] + [piece(2, 2, BLOCK)] * (LEVELS + 3),
             out_specs=[piece(rows), piece(rows)],
             scratch_shapes=[pltpu.VMEM((4, 2, BLOCK, step), jnp.float32)],
         ),
         name="total",
-    )(idx, gown, gprev, *gfars)
+    )(idx, source, gown, *gprevs, *gfars, extra)
 
 
 def spread(x):
@@ -218,23 +276,29 @@
     parts = lax.axis_size("head")
     span = lax.axis_index("seq").astype(jnp.int32).reshape(1)
     used = jnp.stack([jnp.min(block_lists, 0), jnp.max(block_lists, 0)], 1)
-    asked = jnp.stack([passed_along(used[level], -2 * 4**level) for level in range(LEVELS)])
-    own = spread(pack_pair(k_tokens, v_tokens, parts))
-    picked = pick_blocks(asked, own)
-    fars = [None] * LEVELS
-    for level in reversed(range(LEVELS)):
-        fars[level] = passed_along(picked[level], 2 * 4**level)
-    prev = passed_along(own, 1)
-    qd = spread(pack_pair(q_tokens, grad_out, parts))
-    att, grad_q, gown, gprev, *gfars = attend(
-        span, block_lists, block_valid, used, qd, own, prev, fars
+    kv = pack_pair(k_tokens, v_tokens, parts)
+    asked = jnp.stack([passed(used[level], -2 * 4**level) for level in range(LEVELS)])
+    own = spread(kv)
+    qd, asked = lax.optimization_barrier((pack_pair(q_tokens, grad_out, parts), asked))
+    *picked, half0, half1 = pick_blocks(asked, own)
+    far1 = passed(picked[1], 8, True)
+    far0 = passed(picked[0], 2, True)
+    prev0 = passed(half0, 1, True)
+    far2 = passed(picked[2], 32)
+    prev1 = passed(half1, 1)
+    extra, source = relayed(prev0, far0, far1, 1)
+    qd = spread(qd)
+    att, grad_q, gown, gprev0, gprev1, *gfars = attend(
+        span, block_lists, block_valid, used, source, qd, own, (prev0, prev1), (far0, far1, far2), extra
     )
-    back = [None] * LEVELS
-    for level in reversed(range(LEVELS)):
-        back[level] = passed_along(gfars[level], -2 * 4**level)
-    back_prev = passed_along(gprev, -1)
+    back1 = passed(gfars[1], -8, True)
+    back0 = passed(gfars[0], -2, True)
+    bprev0 = passed(gprev0, -1, True)
+    back2 = passed(gfars[2], -32)
+    bprev1 = passed(gprev1, -1)
+    extra, source = relayed(bprev0, back0, back1, -1)
     attended = spread(att).transpose(1, 0, 2).reshape(q_tokens.shape)
-    grad_k, grad_v = total(asked, gown, back_prev, back)
+    grad_k, grad_v = total(asked, source, gown, (bprev0, bprev1), (back0, back1, back2), extra)
     return attended, grad_q, grad_k, grad_v
 
 

time: 275 us -> 203 us (0.74)
  the two profiles are of different devices: /device:TPU:32 before, /device:TPU:126 now
where the time goes in v2:
time: 203 us; the launch traced here: 202 us
  waiting for transfers between devices  94.8 us (47%)
  starting transfers between devices  70.7 us (35%)
  Pallas kernels  29.6 us (15%)
  other arithmetic  3.82 us (2%)
    ppermute x13, waiting for transfers between devices, passed(): return lax.ppermute(shard, 'seq', pairs)  69.1 us
    ppermute x13, starting transfers between devices, passed(): return lax.ppermute(shard, 'seq', pairs)  56.4 us
    ppermute x2, waiting for transfers between devices, stepped(): return lax.ppermute(shard, 'seq', pairs)  25.7 us
    pallas_call x1, Pallas kernels, attend(): pl.pallas_call(attend_body, out_shape=[jax.ShapeDtypeStruct((4, BLOCK, co...  14 us
    all_to_all x3, starting transfers between devices, spread(): return lax.all_to_all(x, 'head', split_axis=0, concat_axis=0)  10.9 us
    pallas_call x2, Pallas kernels, pack_pair(): pl.pallas_call(pack_body, out_shape=jax.ShapeDtypeStruct((parts, 2, rows,...  6.84 us
    pallas_call x1, Pallas kernels, total(): pl.pallas_call(total_body, out_shape=[out, out], grid_spec=pltpu.Prefetch...  5.28 us
  transfers between devices with their start and end apart: 18, of which 7 were waited for; matrix products, arithmetic and copies ran while one was open for 2% of the time, Pallas kernels for 3%

profile of v2, /device:TPU:126, one launch (start us, length us, event | category | flops | bytes accessed | tf_op | source)
XLA Modules:
  0.0 201.6 jit_solution(11307702477030890047)
XLA Ops:
  0.6 0.0 copy-start.12
  0.6 3.4 %pack_pair.3 = bf16[4,2,64,1024]{3,2,1,0:T(8,128)(2,1)} custom-call(bf16[64,4096]{1,0:T(8,128)(2,1)} %a_ref.3, bf16[64,4096]{1,0:T(8,128)(2,1)} %b_ref.3), custom_call_target="tpu_custom_call" | custom-call | tf_op jit(solution)/shard_map/pack_pair/pallas_call | solution.py:72
  4.1 3.6 %all-to-all-start.1 = ((bf16[4,2,64,1024]{3,2,1,0:T(8,128)(2,1)}), bf16[4,2,64,1024]{3,2,1,0:T(8,128)(2,1)S(1)}, u32[]{:S(2)}, u32[]{:S(2)}) async-start(bf16[4,2,64,1024]{3,2,1,0:T(8,128)(2,1)} %pack_pair.3), calls=%async_computation.1 | async-start | bytes 2097152 | tf_op jit(solution)/shard_map/all_to_all | solution.py:272
  7.7 0.1 copy.12
  7.8 0.1 copy.13
  7.9 0.1 pad_add_fusion.used_ref
  8.0 1.3 collective-permute-start.2
  9.2 3.1 %collective-permute-start = (s32[2]{0:T(128)S(1)}, s32[2]{0:T(128)S(1)}, u32[]{:S(2)}, u32[]{:S(2)}) collective-permute-start(s32[2]{0:T(128)S(1)} %get-tuple-element.40), channel_id=1, source_target_pairs={{252,244},{248,240},{244,236},{240,232},{236,228},{232,224},{228,2... | collective-permute-start | bytes 32 | tf_op jit(solution)/shard_map/ppermute | solution.py:38
  12.4 3.3 %collective-permute-start.1 = (s32[2]{0:T(128)S(1)}, s32[2]{0:T(128)S(1)}, u32[]{:S(2)}, u32[]{:S(2)}) collective-permute-start(s32[2]{0:T(128)S(1)} %get-tuple-element.42), channel_id=1, source_target_pairs={{252,220},{248,216},{244,212},{240,208},{236,204},{232,200},{228,1... | collective-permute-start | bytes 32 | tf_op jit(solution)/shard_map/ppermute | solution.py:38
  15.7 3.4 %pack_pair.2 = bf16[4,2,64,1024]{3,2,1,0:T(8,128)(2,1)} custom-call(bf16[64,4096]{1,0:T(8,128)(2,1)} %a_ref.2, bf16[64,4096]{1,0:T(8,128)(2,1)} %b_ref.2), custom_call_target="tpu_custom_call" | custom-call | tf_op jit(solution)/shard_map/pack_pair/pallas_call | solution.py:72
  19.1 6.3 %collective-permute-done.2 = s32[2]{0:T(128)S(1)} collective-permute-done((s32[2]{0:T(128)S(1)}, s32[2]{0:T(128)S(1)}, u32[]{:S(2)}, u32[]{:S(2)}) %collective-permute-start.2) | collective-permute-done | bytes 40 | tf_op jit(solution)/shard_map/ppermute | solution.py:38
  25.5 0.0 collective-permute-done
  25.5 0.6 pad_add_fusion.1.idx_ref
  26.1 0.0 all-to-all-done.1.kv_ref.own_ref
  26.1 3.9 %all-to-all-start = ((bf16[4,2,64,1024]{3,2,1,0:T(8,128)(2,1)}), bf16[4,2,64,1024]{3,2,1,0:T(8,128)(2,1)S(1)}, u32[]{:S(2)}, u32[]{:S(2)}) async-start(bf16[4,2,64,1024]{3,2,1,0:T(8,128)(2,1)} %pack_pair.2), calls=%async_computation | async-start | bytes 2097152 | tf_op jit(solution)/shard_map/all_to_all | solution.py:272
  30.0 3.5 %pick_blocks.1 = (bf16[2,2,64,1024]{3,2,1,0:T(8,128)(2,1)}, bf16[2,2,64,1024]{3,2,1,0:T(8,128)(2,1)}, bf16[2,2,64,1024]{3,2,1,0:T(8,128)(2,1)}, bf16[2,2,64,1024]{3,2,1,0:T(8,128)(2,1)}, bf16[2,2,64,1024]{3,2,1,0:T(8,128)(2,1)}) custom-call(s32[3,2]{1,0:T(4,128)} %pad_add_fusion.1.idx_ref, bf16[4,2,64,1024]{3,2,1,0:T(8,128)(2,1)} %copy-done), custom_call_target="tpu_custom_call" | custom-call | tf_op jit(solution)/shard_map/pick_blocks/pallas_call | solution.py:99
  33.4 2.0 %collective-permute-start.3 = (bf16[2,2,64,1024]{3,2,1,0:T(8,128)(2,1)}, bf16[2,2,64,1024]{3,2,1,0:T(8,128)(2,1)S(1)}, u32[]{:S(2)}, u32[]{:S(2)}) collective-permute-start(bf16[2,2,64,1024]{3,2,1,0:T(8,128)(2,1)} %get-tuple-element.23), channel_id=1, source_target_pairs={{0,4},{4,8},{8,12},{12,16},{16,20},{20,24},{24,28},{28,32},{32,36}... | collective-permute-start | bytes 1572872 | tf_op jit(solution)/shard_map/ppermute | solution.py:38
  35.5 4.5 %collective-permute-start.5 = (bf16[2,2,64,1024]{3,2,1,0:T(8,128)(2,1)}, bf16[2,2,64,1024]{3,2,1,0:T(8,128)(2,1)S(1)}, u32[]{:S(2)}, u32[]{:S(2)}) collective-permute-start(bf16[2,2,64,1024]{3,2,1,0:T(8,128)(2,1)} %get-tuple-element.25), channel_id=1, source_target_pairs={{0,8},{4,12},{8,16},{12,20},{16,24},{20,28},{24,32},{28,36},{32,40... | collective-permute-start | bytes 1572872 | tf_op jit(solution)/shard_map/ppermute | solution.py:38
  40.0 4.3 %collective-permute-start.6 = (bf16[2,2,64,1024]{3,2,1,0:T(8,128)(2,1)}, bf16[2,2,64,1024]{3,2,1,0:T(8,128)(2,1)S(1)}, u32[]{:S(2)}, u32[]{:S(2)}) collective-permute-start(bf16[2,2,64,1024]{3,2,1,0:T(8,128)(2,1)} %get-tuple-element.26), channel_id=1, source_target_pairs={{0,32},{4,36},{8,40},{12,44},{16,48},{20,52},{24,56},{28,60},{32,6... | collective-permute-start | bytes 1572872 | tf_op jit(solution)/shard_map/ppermute | solution.py:38
  44.4 4.0 %collective-permute-start.4 = (bf16[2,2,64,1024]{3,2,1,0:T(8,128)(2,1)}, bf16[2,2,64,1024]{3,2,1,0:T(8,128)(2,1)S(1)}, u32[]{:S(2)}, u32[]{:S(2)}) collective-permute-start(bf16[2,2,64,1024]{3,2,1,0:T(8,128)(2,1)} %get-tuple-element.24), channel_id=1, source_target_pairs={{0,4},{4,8},{8,12},{12,16},{16,20},{20,24},{24,28},{28,32},{32,36}... | collective-permute-start | bytes 1572872 | tf_op jit(solution)/shard_map/ppermute | solution.py:38
  48.4 2.1 %collective-permute-start.7 = (bf16[2,2,64,1024]{3,2,1,0:T(8,128)(2,1)}, bf16[2,2,64,1024]{3,2,1,0:T(8,128)(2,1)}, u32[]{:S(2)}, u32[]{:S(2)}) collective-permute-start(bf16[2,2,64,1024]{3,2,1,0:T(8,128)(2,1)} %get-tuple-element.27), channel_id=1, source_target_pairs={{0,128},{4,132},{8,136},{12,140},{16,144},{20,148},{24,152},{28,15... | collective-permute-start | bytes 1572872 | tf_op jit(solution)/shard_map/ppermute | solution.py:38
  50.5 11.1 %collective-permute-done.3.prev0_ref = bf16[2,2,64,1024]{3,2,1,0:T(8,128)(2,1)S(1)} collective-permute-done((bf16[2,2,64,1024]{3,2,1,0:T(8,128)(2,1)}, bf16[2,2,64,1024]{3,2,1,0:T(8,128)(2,1)S(1)}, u32[]{:S(2)}, u32[]{:S(2)}) %collective-permute-start.3) | collective-permute-done | bytes 524320 | tf_op jit(solution)/shard_map/ppermute | solution.py:38
  61.6 8.8 %collective-permute-done.5.far0_ref = bf16[2,2,64,1024]{3,2,1,0:T(8,128)(2,1)S(1)} collective-permute-done((bf16[2,2,64,1024]{3,2,1,0:T(8,128)(2,1)}, bf16[2,2,64,1024]{3,2,1,0:T(8,128)(2,1)S(1)}, u32[]{:S(2)}, u32[]{:S(2)}) %collective-permute-start.5) | collective-permute-done | bytes 524320 | tf_op jit(solution)/shard_map/ppermute | solution.py:38
  70.4 0.0 collective-permute-done.6.far1_ref
  70.4 0.9 select_select_fusion.1
  71.3 1.4 collective-permute-start.8
  72.8 0.6 pad_add_fusion.2.from_ref
  73.4 0.0 all-to-all-done.qd_ref
  73.4 10.4 %collective-permute-done.4.prev1_ref = bf16[2,2,64,1024]{3,2,1,0:T(8,128)(2,1)S(1)} collective-permute-done((bf16[2,2,64,1024]{3,2,1,0:T(8,128)(2,1)}, bf16[2,2,64,1024]{3,2,1,0:T(8,128)(2,1)S(1)}, u32[]{:S(2)}, u32[]{:S(2)}) %collective-permute-start.4) | collective-permute-done | bytes 524320 | tf_op jit(solution)/shard_map/ppermute | solution.py:38
  83.7 0.0 collective-permute-done.7.far2_ref
  83.8 0.7 copy-done.10
  84.5 14.0 %attend.1 = (bf16[4,64,1024]{2,1,0:T(8,128)(2,1)}, bf16[256,1024]{1,0:T(8,128)(2,1)}, f32[2,256,1024]{2,1,0:T(8,128)}, bf16[2,2,64,1024]{3,2,1,0:T(8,128)(2,1)},...) custom-call(s32[1]{0:T(128)} %bitcast.span_ref, ...), custom_call_target="tpu_custom_call" | custom-call | tf_op jit(solution)/shard_map/attend/pallas_call | solution.py:202
  98.6 2.2 %collective-permute-start.11 = (bf16[2,2,64,1024]{3,2,1,0:T(8,128)(2,1)}, bf16[2,2,64,1024]{3,2,1,0:T(8,128)(2,1)S(1)}, u32[]{:S(2)}, u32[]{:S(2)}) collective-permute-start(bf16[2,2,64,1024]{3,2,1,0:T(8,128)(2,1)} %get-tuple-element.33), channel_id=1, source_target_pairs={{252,244},{248,240},{244,236},{240,232},{236,228},{232,224},{228,2... | collective-permute-start | bytes 1572872 | tf_op jit(solution)/shard_map/ppermute | solution.py:38
  100.8 24.4 %collective-permute-start.12 = (bf16[2,2,64,1024]{3,2,1,0:T(8,128)(2,1)}, bf16[2,2,64,1024]{3,2,1,0:T(8,128)(2,1)S(1)}, u32[]{:S(2)}, u32[]{:S(2)}) collective-permute-start(bf16[2,2,64,1024]{3,2,1,0:T(8,128)(2,1)} %get-tuple-element.34), channel_id=1, source_target_pairs={{252,220},{248,216},{244,212},{240,208},{236,204},{232,200},{228,1... | collective-permute-start | bytes 1572872 | tf_op jit(solution)/shard_map/ppermute | solution.py:38
  125.1 1.9 collective-permute-start.9
  127.1 1.9 collective-permute-start.10
  129.0 1.3 collective-permute-start.13
  130.3 3.5 %all-to-all-start.2 = ((bf16[4,64,1024]{2,1,0:T(8,128)(2,1)}), bf16[4,64,1024]{2,1,0:T(8,128)(2,1)S(1)}, u32[]{:S(2)}, u32[]{:S(2)}) async-start(bf16[4,64,1024]{2,1,0:T(8,128)(2,1)} %get-tuple-element.28), calls=%async_computation.2 | async-start | bytes 1048576 | tf_op jit(solution)/shard_map/all_to_all | solution.py:272
  133.8 30.9 %collective-permute-done.11.gfar0_ref = bf16[2,2,64,1024]{3,2,1,0:T(8,128)(2,1)S(1)} collective-permute-done((bf16[2,2,64,1024]{3,2,1,0:T(8,128)(2,1)}, bf16[2,2,64,1024]{3,2,1,0:T(8,128)(2,1)S(1)}, u32[]{:S(2)}, u32[]{:S(2)}) %collective-permute-start.11) | collective-permute-done | bytes 524320 | tf_op jit(solution)/shard_map/ppermute | solution.py:38
  164.7 0.0 collective-permute-done.12.gfar1_ref
  164.7 1.5 collective-permute-done.9.gprev0_ref
  166.2 1.0 select_select_fusion
  167.2 1.9 collective-permute-start.14
  169.1 0.6 pad_add_fusion.3.from_ref
  169.8 0.0 all-to-all-done.2
  169.8 0.8 copy.15
  170.6 25.7 %collective-permute-done.14.extra_ref = bf16[2,2,64,1024]{3,2,1,0:T(8,128)(2,1)} collective-permute-done((bf16[2,2,64,1024]{3,2,1,0:T(8,128)(2,1)}, bf16[2,2,64,1024]{3,2,1,0:T(8,128)(2,1)}, u32[]{:S(2)}, u32[]{:S(2)}) %collective-permute-start.14) | collective-permute-done | bytes 524320 | tf_op jit(solution)/shard_map/ppermute | solution.py:47
  196.4 5.3 %total.1 = (bf16[256,1024]{1,0:T(8,128)(2,1)}, bf16[256,1024]{1,0:T(8,128)(2,1)}) custom-call(s32[3,2]{1,0:T(4,128)} %pad_add_fusion.1.idx_ref, s32[3]{0:T(128)} %pad_add_fusion.3.from_ref, f32[2,256,1024]{2,1,0:T(8,128)} %get-tuple-element.30.gown_ref, bf16[2,2,64,1024]{3,2,1,0:T(8,128)(2,1)} %copy-done.6, bf16[2,2,64,1024]{3,2,1,0:T(8,128)(2,1)} %copy-done.8, ...), custom_call_target="tpu_custom_call" | custom-call | tf_op jit(solution)/shard_map/total/pallas_call | solution.py:257
  (30 shorter events, 0.1 us)
Async XLA Ops:
  0.6 7.0 %copy-start.12 = (s32[4,3]{1,0:T(4,128)S(1)}, s32[4,3]{1,0:T(4,128)}, u32[]{:S(2)}) copy-start(s32[4,3]{1,0:T(4,128)} %lists_ref.1) | copy-start | bytes 148
  4.1 22.0 %all-to-all-start.1 = ((bf16[4,2,64,1024]{3,2,1,0:T(8,128)(2,1)}), bf16[4,2,64,1024]{3,2,1,0:T(8,128)(2,1)S(1)}, u32[]{:S(2)}, u32[]{:S(2)}) async-start(bf16[4,2,64,1024]{3,2,1,0:T(8,128)(2,1)} %pack_pair.3), calls=%async_computation.1 | async-start | bytes 2097152 | tf_op jit(solution)/shard_map/all_to_all | solution.py:272
  7.9 18.1 %copy-start.11 = (s32[3,2]{1,0:T(4,128)}, s32[3,2]{1,0:T(4,128)S(1)}, u32[]{:S(2)}) copy-start(s32[3,2]{1,0:T(4,128)S(1)} %pad_add_fusion.used_ref) | copy-start | bytes 76
  8.0 17.5 %collective-permute-start.2 = (s32[2]{0:T(128)S(1)}, s32[2]{0:T(128)S(1)}, u32[]{:S(2)}, u32[]{:S(2)}) collective-permute-start(s32[2]{0:T(128)S(1)} %get-tuple-element.41), channel_id=1, source_target_pairs={{252,124},{248,120},{244,116},{240,112},{236,108},{232,104},{228,1... | collective-permute-start | bytes 32 | tf_op jit(solution)/shard_map/ppermute | solution.py:38
  9.2 16.2 %collective-permute-start = (s32[2]{0:T(128)S(1)}, s32[2]{0:T(128)S(1)}, u32[]{:S(2)}, u32[]{:S(2)}) collective-permute-start(s32[2]{0:T(128)S(1)} %get-tuple-element.40), channel_id=1, source_target_pairs={{252,244},{248,240},{244,236},{240,232},{236,228},{232,224},{228,2... | collective-permute-start | bytes 32 | tf_op jit(solution)/shard_map/ppermute | solution.py:38
  12.4 13.1 %collective-permute-start.1 = (s32[2]{0:T(128)S(1)}, s32[2]{0:T(128)S(1)}, u32[]{:S(2)}, u32[]{:S(2)}) collective-permute-start(s32[2]{0:T(128)S(1)} %get-tuple-element.42), channel_id=1, source_target_pairs={{252,220},{248,216},{244,212},{240,208},{236,204},{232,200},{228,1... | collective-permute-start | bytes 32 | tf_op jit(solution)/shard_map/ppermute | solution.py:38
  26.1 3.9 %copy-start = (bf16[4,2,64,1024]{3,2,1,0:T(8,128)(2,1)}, bf16[4,2,64,1024]{3,2,1,0:T(8,128)(2,1)S(1)}, u32[]{:S(2)}) copy-start(bf16[4,2,64,1024]{3,2,1,0:T(8,128)(2,1)S(1)} %all-to-all-done.1.kv_ref.own_ref) | copy-start | bytes 3145732
  26.1 47.3 %all-to-all-start = ((bf16[4,2,64,1024]{3,2,1,0:T(8,128)(2,1)}), bf16[4,2,64,1024]{3,2,1,0:T(8,128)(2,1)S(1)}, u32[]{:S(2)}, u32[]{:S(2)}) async-start(bf16[4,2,64,1024]{3,2,1,0:T(8,128)(2,1)} %pack_pair.2), calls=%async_computation | async-start | bytes 2097152 | tf_op jit(solution)/shard_map/all_to_all | solution.py:272
  33.4 28.1 %collective-permute-start.3 = (bf16[2,2,64,1024]{3,2,1,0:T(8,128)(2,1)}, bf16[2,2,64,1024]{3,2,1,0:T(8,128)(2,1)S(1)}, u32[]{:S(2)}, u32[]{:S(2)}) collective-permute-start(bf16[2,2,64,1024]{3,2,1,0:T(8,128)(2,1)} %get-tuple-element.23), channel_id=1, source_target_pairs={{0,4},{4,8},{8,12},{12,16},{16,20},{20,24},{24,28},{28,32},{32,36}... | collective-permute-start | bytes 1572872 | tf_op jit(solution)/shard_map/ppermute | solution.py:38
  35.5 34.9 %collective-permute-start.5 = (bf16[2,2,64,1024]{3,2,1,0:T(8,128)(2,1)}, bf16[2,2,64,1024]{3,2,1,0:T(8,128)(2,1)S(1)}, u32[]{:S(2)}, u32[]{:S(2)}) collective-permute-start(bf16[2,2,64,1024]{3,2,1,0:T(8,128)(2,1)} %get-tuple-element.25), channel_id=1, source_target_pairs={{0,8},{4,12},{8,16},{12,20},{16,24},{20,28},{24,32},{28,36},{32,40... | collective-permute-start | bytes 1572872 | tf_op jit(solution)/shard_map/ppermute | solution.py:38
  40.0 30.4 %collective-permute-start.6 = (bf16[2,2,64,1024]{3,2,1,0:T(8,128)(2,1)}, bf16[2,2,64,1024]{3,2,1,0:T(8,128)(2,1)S(1)}, u32[]{:S(2)}, u32[]{:S(2)}) collective-permute-start(bf16[2,2,64,1024]{3,2,1,0:T(8,128)(2,1)} %get-tuple-element.26), channel_id=1, source_target_pairs={{0,32},{4,36},{8,40},{12,44},{16,48},{20,52},{24,56},{28,60},{32,6... | collective-permute-start | bytes 1572872 | tf_op jit(solution)/shard_map/ppermute | solution.py:38
  44.4 39.4 %collective-permute-start.4 = (bf16[2,2,64,1024]{3,2,1,0:T(8,128)(2,1)}, bf16[2,2,64,1024]{3,2,1,0:T(8,128)(2,1)S(1)}, u32[]{:S(2)}, u32[]{:S(2)}) collective-permute-start(bf16[2,2,64,1024]{3,2,1,0:T(8,128)(2,1)} %get-tuple-element.24), channel_id=1, source_target_pairs={{0,4},{4,8},{8,12},{12,16},{16,20},{20,24},{24,28},{28,32},{32,36}... | collective-permute-start | bytes 1572872 | tf_op jit(solution)/shard_map/ppermute | solution.py:38
  48.4 35.4 %collective-permute-start.7 = (bf16[2,2,64,1024]{3,2,1,0:T(8,128)(2,1)}, bf16[2,2,64,1024]{3,2,1,0:T(8,128)(2,1)}, u32[]{:S(2)}, u32[]{:S(2)}) collective-permute-start(bf16[2,2,64,1024]{3,2,1,0:T(8,128)(2,1)} %get-tuple-element.27), channel_id=1, source_target_pairs={{0,128},{4,132},{8,136},{12,140},{16,144},{20,148},{24,152},{28,15... | collective-permute-start | bytes 1572872 | tf_op jit(solution)/shard_map/ppermute | solution.py:38
  61.6 22.2 %copy-start.3 = (bf16[2,2,64,1024]{3,2,1,0:T(8,128)(2,1)}, bf16[2,2,64,1024]{3,2,1,0:T(8,128)(2,1)S(1)}, u32[]{:S(2)}) copy-start(bf16[2,2,64,1024]{3,2,1,0:T(8,128)(2,1)S(1)} %collective-permute-done.3.prev0_ref) | copy-start | bytes 1572868
  70.4 13.4 %copy-start.5 = (bf16[2,2,64,1024]{3,2,1,0:T(8,128)(2,1)}, bf16[2,2,64,1024]{3,2,1,0:T(8,128)(2,1)S(1)}, u32[]{:S(2)}) copy-start(bf16[2,2,64,1024]{3,2,1,0:T(8,128)(2,1)S(1)} %collective-permute-done.5.far0_ref) | copy-start | bytes 1572868
  70.4 13.4 %copy-start.7 = (bf16[2,2,64,1024]{3,2,1,0:T(8,128)(2,1)}, bf16[2,2,64,1024]{3,2,1,0:T(8,128)(2,1)S(1)}, u32[]{:S(2)}) copy-start(bf16[2,2,64,1024]{3,2,1,0:T(8,128)(2,1)S(1)} %collective-permute-done.6.far1_ref) | copy-start | bytes 1572868
  71.3 12.4 %collective-permute-start.8 = (bf16[2,2,64,1024]{3,2,1,0:T(8,128)(2,1)}, bf16[2,2,64,1024]{3,2,1,0:T(8,128)(2,1)}, u32[]{:S(2)}, u32[]{:S(2)}) collective-permute-start(bf16[2,2,64,1024]{3,2,1,0:T(8,128)(2,1)} %select_select_fusion.1), channel_id=1, source_target_pairs={{0,64},{4,68},{24,88},{28,92},{64,128},{68,132},{88,152},{92,156},... | collective-permute-start | bytes 1572872 | tf_op jit(solution)/shard_map/ppermute | solution.py:47
  73.4 10.4 %copy-start.1 = (bf16[4,2,64,1024]{3,2,1,0:T(8,128)(2,1)}, bf16[4,2,64,1024]{3,2,1,0:T(8,128)(2,1)S(1)}, u32[]{:S(2)}) copy-start(bf16[4,2,64,1024]{3,2,1,0:T(8,128)(2,1)S(1)} %all-to-all-done.qd_ref) | copy-start | bytes 3145732
  83.7 0.8 copy-start.10
  98.6 66.1 %collective-permute-start.11 = (bf16[2,2,64,1024]{3,2,1,0:T(8,128)(2,1)}, bf16[2,2,64,1024]{3,2,1,0:T(8,128)(2,1)S(1)}, u32[]{:S(2)}, u32[]{:S(2)}) collective-permute-start(bf16[2,2,64,1024]{3,2,1,0:T(8,128)(2,1)} %get-tuple-element.33), channel_id=1, source_target_pairs={{252,244},{248,240},{244,236},{240,232},{236,228},{232,224},{228,2... | collective-permute-start | bytes 1572872 | tf_op jit(solution)/shard_map/ppermute | solution.py:38
  100.8 64.0 %collective-permute-start.12 = (bf16[2,2,64,1024]{3,2,1,0:T(8,128)(2,1)}, bf16[2,2,64,1024]{3,2,1,0:T(8,128)(2,1)S(1)}, u32[]{:S(2)}, u32[]{:S(2)}) collective-permute-start(bf16[2,2,64,1024]{3,2,1,0:T(8,128)(2,1)} %get-tuple-element.34), channel_id=1, source_target_pairs={{252,220},{248,216},{244,212},{240,208},{236,204},{232,200},{228,1... | collective-permute-start | bytes 1572872 | tf_op jit(solution)/shard_map/ppermute | solution.py:38
  125.1 41.1 %collective-permute-start.9 = (bf16[2,2,64,1024]{3,2,1,0:T(8,128)(2,1)}, bf16[2,2,64,1024]{3,2,1,0:T(8,128)(2,1)S(1)}, u32[]{:S(2)}, u32[]{:S(2)}) collective-permute-start(bf16[2,2,64,1024]{3,2,1,0:T(8,128)(2,1)} %get-tuple-element.31), channel_id=1, source_target_pairs={{252,248},{248,244},{244,240},{240,236},{236,232},{232,228},{228,2... | collective-permute-start | bytes 1572872 | tf_op jit(solution)/shard_map/ppermute | solution.py:38
  127.1 43.5 %collective-permute-start.10 = (bf16[2,2,64,1024]{3,2,1,0:T(8,128)(2,1)}, bf16[2,2,64,1024]{3,2,1,0:T(8,128)(2,1)S(1)}, u32[]{:S(2)}, u32[]{:S(2)}) collective-permute-start(bf16[2,2,64,1024]{3,2,1,0:T(8,128)(2,1)} %get-tuple-element.32), channel_id=1, source_target_pairs={{252,248},{248,244},{244,240},{240,236},{236,232},{232,228},{228,2... | collective-permute-start | bytes 1572872 | tf_op jit(solution)/shard_map/ppermute | solution.py:38
  129.0 41.6 %collective-permute-start.13 = (bf16[2,2,64,1024]{3,2,1,0:T(8,128)(2,1)}, bf16[2,2,64,1024]{3,2,1,0:T(8,128)(2,1)S(1)}, u32[]{:S(2)}, u32[]{:S(2)}) collective-permute-start(bf16[2,2,64,1024]{3,2,1,0:T(8,128)(2,1)} %get-tuple-element.35), channel_id=1, source_target_pairs={{252,124},{248,120},{244,116},{240,112},{236,108},{232,104},{228,1... | collective-permute-start | bytes 1572872 | tf_op jit(solution)/shard_map/ppermute | solution.py:38
  130.3 39.5 %all-to-all-start.2 = ((bf16[4,64,1024]{2,1,0:T(8,128)(2,1)}), bf16[4,64,1024]{2,1,0:T(8,128)(2,1)S(1)}, u32[]{:S(2)}, u32[]{:S(2)}) async-start(bf16[4,64,1024]{2,1,0:T(8,128)(2,1)} %get-tuple-element.28), calls=%async_computation.2 | async-start | bytes 1048576 | tf_op jit(solution)/shard_map/all_to_all | solution.py:272
  164.7 31.6 %copy-start.2 = (bf16[2,2,64,1024]{3,2,1,0:T(8,128)(2,1)}, bf16[2,2,64,1024]{3,2,1,0:T(8,128)(2,1)S(1)}, u32[]{:S(2)}) copy-start(bf16[2,2,64,1024]{3,2,1,0:T(8,128)(2,1)S(1)} %collective-permute-done.11.gfar0_ref) | copy-start | bytes 1572868
  164.7 31.6 %copy-start.4 = (bf16[2,2,64,1024]{3,2,1,0:T(8,128)(2,1)}, bf16[2,2,64,1024]{3,2,1,0:T(8,128)(2,1)S(1)}, u32[]{:S(2)}) copy-start(bf16[2,2,64,1024]{3,2,1,0:T(8,128)(2,1)S(1)} %collective-permute-done.12.gfar1_ref) | copy-start | bytes 1572868
  166.2 30.1 %copy-start.6 = (bf16[2,2,64,1024]{3,2,1,0:T(8,128)(2,1)}, bf16[2,2,64,1024]{3,2,1,0:T(8,128)(2,1)S(1)}, u32[]{:S(2)}) copy-start(bf16[2,2,64,1024]{3,2,1,0:T(8,128)(2,1)S(1)} %collective-permute-done.9.gprev0_ref) | copy-start | bytes 1572868
  167.2 29.2 %collective-permute-start.14 = (bf16[2,2,64,1024]{3,2,1,0:T(8,128)(2,1)}, bf16[2,2,64,1024]{3,2,1,0:T(8,128)(2,1)}, u32[]{:S(2)}, u32[]{:S(2)}) collective-permute-start(bf16[2,2,64,1024]{3,2,1,0:T(8,128)(2,1)} %select_select_fusion), channel_id=1, source_target_pairs={{252,188},{248,184},{228,164},{224,160},{188,124},{184,120},{164,1... | collective-permute-start | bytes 1572872 | tf_op jit(solution)/shard_map/ppermute | solution.py:47
  170.6 25.7 %copy-start.8 = (bf16[2,2,64,1024]{3,2,1,0:T(8,128)(2,1)}, bf16[2,2,64,1024]{3,2,1,0:T(8,128)(2,1)S(1)}, u32[]{:S(2)}) copy-start(bf16[2,2,64,1024]{3,2,1,0:T(8,128)(2,1)S(1)} %collective-permute-done.10.gprev1_ref) | copy-start | bytes 1572868
  170.6 25.7 %copy-start.9 = (bf16[2,2,64,1024]{3,2,1,0:T(8,128)(2,1)}, bf16[2,2,64,1024]{3,2,1,0:T(8,128)(2,1)S(1)}, u32[]{:S(2)}) copy-start(bf16[2,2,64,1024]{3,2,1,0:T(8,128)(2,1)S(1)} %collective-permute-done.13.gfar2_ref) | copy-start | bytes 1572868

commit v3 on v2

v3 whole, which is shorter than its diff:
```python
import functools

import jax
import jax.numpy as jnp
from jax import lax
from jax.experimental import pallas as pl
from jax.experimental.pallas import tpu as pltpu
from jax.sharding import PartitionSpec as P


HEAD_DIM = 128
WINDOW = 256
BLOCK = 64
LEVELS = 3
NEG = -1e30


DETOURS = {1: {15: 0}, 2: {15: 1}, 8: {14: 6, 15: 7}}
PLANE = 16


def pairs_of(peers, by, detour):
    pairs = []
    for i in range(peers):
        if i + by < peers:
            to = i + by
            if detour and to // PLANE > i // PLANE:
                at = DETOURS[by].get(i % PLANE)
                to = to if at is None else i // PLANE * PLANE + at
            pairs.append((i, to))
    return pairs


def passed(shard, by, detour=False):
    peers = lax.axis_size("seq")
    pairs = pairs_of(peers, abs(by), detour)
    if by < 0:
        pairs = [(peers - 1 - i, peers - 1 - j) for i, j in pairs]
    return lax.ppermute(shard, "seq", pairs)


def stepped(shard, by):
    peers = lax.axis_size("seq")
    relays = list(DETOURS[abs(by)].values())
    pairs = [(i, i + PLANE) for i in range(peers - PLANE) if i % PLANE in relays]
    at = lax.axis_index("seq")
    if by < 0:
        pairs = [(peers - 1 - i, peers - 1 - j) for i, j in pairs]
        at = peers - 1 - at
    hit = functools.reduce(jnp.logical_or, [at % PLANE == v for v in relays])
    source = jnp.where(hit, jnp.where(at >= PLANE, 1, 2), 0).astype(jnp.int32)
    return lax.ppermute(shard, "seq", pairs), source


def pack_body(a_ref, b_ref, out_ref):
    out_ref[0, 0] = a_ref[...]
    out_ref[0, 1] = b_ref[...]


def pack_pair(a, b, parts):
    rows, cols = a.shape
    piece = pl.BlockSpec((rows, cols // parts), lambda i: (0, i))
    return pl.pallas_call(
        pack_body,
        out_shape=jax.ShapeDtypeStruct((parts, 2, rows, cols // parts), a.dtype),
        grid=(parts,),
        in_specs=[piece, piece],
        out_specs=pl.BlockSpec((1, 2, rows, cols // parts), lambda i: (i, 0, 0, 0)),
        name="pack_pair",
    )(a, b)


def pick_body(idx_ref, kv_ref, *rest):
    outs, sems = rest[:-1], rest[-1]
    copies = []
    for level in range(LEVELS):
        for slot in range(2):
            copies.append((kv_ref.at[idx_ref[level, slot]], outs[level].at[slot]))
    copies.append((kv_ref.at[:2], outs[LEVELS]))
    copies.append((kv_ref.at[2:], outs[LEVELS + 1]))
    copies = [pltpu.make_async_copy(src, dst, sems.at[n]) for n, (src, dst) in enumerate(copies)]
    for copy in copies:
        copy.start()
    for copy in copies:
        copy.wait()


def pick_blocks(idx, kv):
    shape = jax.ShapeDtypeStruct((2,) + kv.shape[1:], kv.dtype)
    return pl.pallas_call(
        pick_body,
        out_shape=[shape] * (LEVELS + 2),
        grid_spec=pltpu.PrefetchScalarGridSpec(
            num_scalar_prefetch=1,
            in_specs=[pl.BlockSpec(memory_space=pltpu.VMEM)],
            out_specs=[pl.BlockSpec(memory_space=pl.ANY)] * (LEVELS + 2),
            grid=(1,),
            scratch_shapes=[pltpu.SemaphoreType.DMA((2 * LEVELS + 2,))],
        ),
        name="pick_blocks",
    )(idx, kv)


def dot_nt(a, b):
    return lax.dot_general(a, b, (((1,), (1,)), ((), ())), preferred_element_type=jnp.float32)


def dot_nn(a, b):
    return lax.dot_general(a, b, (((1,), (0,)), ((), ())), preferred_element_type=jnp.float32)


def dot_tn(a, b):
    return lax.dot_general(a, b, (((0,), (0,)), ((), ())), preferred_element_type=jnp.float32)


PAIR = 2


def attend_body(
    span_ref, lists_ref, valid_ref, used_ref, from_ref,
    qd_ref, own_ref, prev0_ref, prev1_ref, far0_ref, far1_ref, far2_ref, *rest,
):
    extra_refs = rest[:3]
    (
    att_ref, ds_ref, wb_ref, gprev0_ref, gprev1_ref, gfar0_ref, gfar1_ref, gfar2_ref,
    bias_ref, k_ref, v_ref,
    ) = rest[3:]
    rows = 4 * BLOCK
    near = WINDOW + rows
    scale = HEAD_DIM ** -0.5
    bf = jnp.bfloat16

    @pl.when(pl.program_id(0) == 0)
    def _():
        first = span_ref[0] == 0
        i = lax.broadcasted_iota(jnp.int32, (rows, near), 0)
        j = lax.broadcasted_iota(jnp.int32, (rows, near), 1)
        low = jnp.where(first, WINDOW, 0)
        ok = (j > i) & (j <= i + WINDOW) & (j >= low)
        bias_ref[:, :near] = jnp.where(ok, 0.0, NEG)
        for b in range(4):
            for level in range(LEVELS):
                for slot in range(2):
                    hit = (valid_ref[b, level] > 0) & (lists_ref[b, level] == used_ref[level, slot])
                    value = jnp.where(hit, 0.0, NEG)
                    at = near + (level * 2 + slot) * BLOCK
                    bias_ref[b * BLOCK:(b + 1) * BLOCK, at:at + BLOCK] = jnp.full(
                        (BLOCK, BLOCK), value, jnp.float32
                    )

    heads = range(PAIR)
    lanes = [slice(n * HEAD_DIM, (n + 1) * HEAD_DIM) for n in heads]

    for n in heads:
        at = 0
        for ref, blocks, source in (
            (prev0_ref, 2, 0), (prev1_ref, 2, None), (own_ref, 4, None),
            (far0_ref, 2, 1), (far1_ref, 2, 2), (far2_ref, 2, None),
        ):
            for b in range(blocks):
                for which, out in enumerate((k_ref, v_ref)):
                    block = ref[b, which, :, lanes[n]]
                    if source is not None:
                        other = extra_refs[source][b, which, :, lanes[n]]
                        block = jnp.where(from_ref[source] == 1, other, block)
                    out[n, at:at + BLOCK, :] = block
                at += BLOCK
    q = [qd_ref[:, 0, :, lanes[n]].reshape(rows, HEAD_DIM) for n in heads]
    d = [qd_ref[:, 1, :, lanes[n]].reshape(rows, HEAD_DIM) for n in heads]
    s = [dot_nt(q[n], k_ref[n]) for n in heads]
    w, wb, dp = [None] * PAIR, [None] * PAIR, [None] * PAIR
    for n in heads:
        dp[n] = dot_nt(d[n], v_ref[n])
        t = s[n] * scale + bias_ref[...]
        p = jnp.exp(t - jnp.max(t, -1, keepdims=True))
        w[n] = p * (1.0 / jnp.sum(p, -1, keepdims=True))
        wb[n] = w[n].astype(bf)
    for n in heads:
        att = dot_nn(wb[n], v_ref[n]).astype(bf)
        att_ref[:, :, lanes[n]] = att.reshape(4, BLOCK, HEAD_DIM)
        delta = jnp.sum(d[n].astype(jnp.float32) * att.astype(jnp.float32), -1, keepdims=True)
        ds = (w[n] * (dp[n] - delta)).astype(bf)
        ds_ref[n] = ds
        wb_ref[n] = wb[n][:, WINDOW:near]
        for a, c, refs in (
            (0, WINDOW, (gprev0_ref, gprev1_ref)),
            (near, near + 2 * LEVELS * BLOCK, (gfar0_ref, gfar1_ref, gfar2_ref)),
        ):
            gv = dot_tn(wb[n][:, a:c], d[n])
            gk = dot_tn(ds[:, a:c], q[n]) * scale
            for part, ref in enumerate(refs):
                at = slice(2 * part * BLOCK, 2 * (part + 1) * BLOCK)
                ref[:, 0, :, lanes[n]] = gk[at].astype(bf).reshape(2, BLOCK, HEAD_DIM)
                ref[:, 1, :, lanes[n]] = gv[at].astype(bf).reshape(2, BLOCK, HEAD_DIM)


def attend(span, lists, valid, used, source, qd, own, prevs, fars, extras):
    cols = qd.shape[-1]
    step = PAIR * HEAD_DIM
    rows = 4 * BLOCK
    keys = WINDOW + rows + 2 * LEVELS * BLOCK

    def piece(*lead):
        return pl.BlockSpec(lead + (step,), lambda h, *_: (0,) * len(lead) + (h,))

    def when_sent(n):
        return pl.BlockSpec(
            (2, 2, BLOCK, step), lambda h, a, b, c, d, source: (0, 0, 0, jnp.where(source[n] == 1, h, 0))
        )

    def per_head(width):
        return pl.BlockSpec((PAIR, rows, width), lambda h, *_: (h, 0, 0))

    four, two = piece(4, 2, BLOCK), piece(2, 2, BLOCK)
    bf = jnp.bfloat16
    return pl.pallas_call(
        attend_body,
        out_shape=[
            jax.ShapeDtypeStruct((4, BLOCK, cols), bf),
            jax.ShapeDtypeStruct((cols // HEAD_DIM, rows, keys), bf),
            jax.ShapeDtypeStruct((cols // HEAD_DIM, rows, rows), bf),
        ] + [jax.ShapeDtypeStruct((2, 2, BLOCK, cols), bf)] * (LEVELS + 2),
        grid_spec=pltpu.PrefetchScalarGridSpec(
            num_scalar_prefetch=5,
            grid=(cols // step,),
            in_specs=[four, four] + [two] * (LEVELS + 2) + [when_sent(n) for n in range(3)],
            out_specs=[piece(4, BLOCK), per_head(keys), per_head(rows)] + [two] * (LEVELS + 2),
            scratch_shapes=[
                pltpu.VMEM((rows, keys), jnp.float32),
                pltpu.VMEM((PAIR, keys, HEAD_DIM), bf),
                pltpu.VMEM((PAIR, keys, HEAD_DIM), bf),
            ],
        ),
        name="attend",
    )(span, lists, valid, used, source, qd, own, *prevs, *fars, *extras)


def own_body(
    from_ref, qd_ref, own_ref, prev0_ref, prev1_ref, far0_ref, far1_ref, far2_ref, *rest,
):
    extra_refs, (ds_ref, wb_ref, gq_ref, gown_ref, k_ref) = rest[:3], rest[3:]
    rows = 4 * BLOCK
    near = WINDOW + rows
    scale = HEAD_DIM ** -0.5
    for n in range(PAIR):
        lanes = slice(n * HEAD_DIM, (n + 1) * HEAD_DIM)
        at = 0
        for ref, blocks, source in (
            (prev0_ref, 2, 0), (prev1_ref, 2, None), (own_ref, 4, None),
            (far0_ref, 2, 1), (far1_ref, 2, 2), (far2_ref, 2, None),
        ):
            for b in range(blocks):
                block = ref[b, 0, :, lanes]
                if source is not None:
                    block = jnp.where(from_ref[source] == 1, extra_refs[source][b, 0, :, lanes], block)
                k_ref[n, at:at + BLOCK, :] = block
                at += BLOCK
        q = qd_ref[:, 0, :, lanes].reshape(rows, HEAD_DIM)
        d = qd_ref[:, 1, :, lanes].reshape(rows, HEAD_DIM)
        ds = ds_ref[n]
        gq_ref[:, lanes] = (dot_nn(ds, k_ref[n]) * scale).astype(jnp.bfloat16)
        gown_ref[0, :, lanes] = dot_tn(ds[:, WINDOW:near], q) * scale
        gown_ref[1, :, lanes] = dot_tn(wb_ref[n], d)


def own_grads(source, qd, own, prevs, fars, extras, ds, wb):
    cols = qd.shape[-1]
    step = PAIR * HEAD_DIM
    rows = 4 * BLOCK
    keys = ds.shape[-1]

    def piece(*lead):
        return pl.BlockSpec(lead + (step,), lambda h, *_: (0,) * len(lead) + (h,))

    def keys_of(blocks):
        return pl.BlockSpec((blocks, 1, BLOCK, step), lambda h, *_: (0, 0, 0, h))

    def per_head(width):
        return pl.BlockSpec((PAIR, rows, width), lambda h, *_: (h, 0, 0))

    return pl.pallas_call(
        own_body,
        out_shape=[
            jax.ShapeDtypeStruct((rows, cols), jnp.bfloat16),
            jax.ShapeDtypeStruct((2, rows, cols), jnp.float32),
        ],
        grid_spec=pltpu.PrefetchScalarGridSpec(
            num_scalar_prefetch=1,
            grid=(cols // step,),
            in_specs=[piece(4, 2, BLOCK), keys_of(4)] + [keys_of(2)] * (LEVELS + 5) + [per_head(keys), per_head(rows)],
            out_specs=[piece(rows), piece(2, rows)],
            scratch_shapes=[pltpu.VMEM((PAIR, keys, HEAD_DIM), jnp.bfloat16)],
        ),
        name="own_grads",
    )(source, qd, own, *prevs, *fars, *extras, ds, wb)


def total_body(
    idx_ref, from_ref, gown_ref, gprev0_ref, gprev1_ref, gfar0_ref, gfar1_ref, gfar2_ref,
    extra0_ref, extra1_ref, extra2_ref, gk_ref, gv_ref, acc_ref,
):
    extra_refs = (extra0_ref, extra1_ref, extra2_ref)

    def part(ref, slot, source):
        block = ref[slot].astype(jnp.float32)
        if source is not None:
            other = extra_refs[source][slot].astype(jnp.float32)
            own = from_ref[source]
            block = jnp.where(own == 0, block, jnp.where(own == 1, other, 0.0))
        return block

    for b in range(4):
        rows = slice(b * BLOCK, (b + 1) * BLOCK)
        acc_ref[b] = gown_ref[:, rows] + (part(gprev0_ref, b, 0) if b < 2 else part(gprev1_ref, b - 2, None))
    for level, (ref, source) in enumerate(((gfar0_ref, 1), (gfar1_ref, 2), (gfar2_ref, None))):
        for slot in range(2):
            at = idx_ref[level, slot]
            acc_ref[at] += part(ref, slot, source)
    for b in range(4):
        gk_ref[b * BLOCK:(b + 1) * BLOCK, :] = acc_ref[b, 0].astype(jnp.bfloat16)
        gv_ref[b * BLOCK:(b + 1) * BLOCK, :] = acc_ref[b, 1].astype(jnp.bfloat16)


def total(idx, source, gown, gprevs, gfars, extras):
    cols = gown.shape[-1]
    rows = 4 * BLOCK
    step = 512

    def piece(*lead):
        return pl.BlockSpec(lead + (step,), lambda h, *_: (0,) * len(lead) + (h,))

    def when_sent(n):
        return pl.BlockSpec((2, 2, BLOCK, step), lambda h, idx, source: (0, 0, 0, jnp.where(source[n] == 1, h, 0)))

    out = jax.ShapeDtypeStruct((rows, cols), jnp.bfloat16)
    return pl.pallas_call(
        total_body,
        out_shape=[out, out],
        grid_spec=pltpu.PrefetchScalarGridSpec(
            num_scalar_prefetch=2,
            grid=(cols // step,),
            in_specs=[piece(2, rows)] + [piece(2, 2, BLOCK)] * (LEVELS + 2) + [when_sent(n) for n in range(3)],
            out_specs=[piece(rows), piece(rows)],
            scratch_shapes=[pltpu.VMEM((4, 2, BLOCK, step), jnp.float32)],
        ),
        name="total",
    )(idx, source, gown, *gprevs, *gfars, *extras)


def spread(x):
    return lax.all_to_all(x, "head", split_axis=0, concat_axis=0)


def second_steps(sign, *shards):
    pieces = [stepped(shard, sign * by) for by, shard in zip((1, 2, 8), shards)]
    return [piece for piece, _ in pieces], jnp.stack([source for _, source in pieces])


def per_device(q_tokens, k_tokens, v_tokens, grad_out, block_lists, block_valid):
    parts = lax.axis_size("head")
    span = lax.axis_index("seq").astype(jnp.int32).reshape(1)
    used = jnp.stack([jnp.min(block_lists, 0), jnp.max(block_lists, 0)], 1)
    kv = pack_pair(k_tokens, v_tokens, parts)
    asked = jnp.stack([passed(used[level], -2 * 4**level) for level in range(LEVELS)])
    own = spread(kv)
    qd, asked = lax.optimization_barrier((pack_pair(q_tokens, grad_out, parts), asked))
    *picked, half0, half1 = pick_blocks(asked, own)
    qd = spread(qd)
    far0 = passed(picked[0], 2, True)
    prev0 = passed(half0, 1, True)
    far1 = passed(picked[1], 8, True)
    far2 = passed(picked[2], 32)
    prev1 = passed(half1, 1)
    extras, source = second_steps(1, prev0, far0, far1)
    att, ds, wb, gprev0, gprev1, *gfars = attend(
        span, block_lists, block_valid, used, source, qd, own, (prev0, prev1), (far0, far1, far2), extras
    )
    back0 = passed(gfars[0], -2, True)
    bprev0 = passed(gprev0, -1, True)
    back1 = passed(gfars[1], -8, True)
    back2 = passed(gfars[2], -32)
    bprev1 = passed(gprev1, -1)
    bextras, bsource = second_steps(-1, bprev0, back0, back1)
    att = spread(att)
    grad_q, gown = own_grads(source, qd, own, (prev0, prev1), (far0, far1, far2), extras, ds, wb)
    attended = att.transpose(1, 0, 2).reshape(q_tokens.shape)
    grad_k, grad_v = total(asked, bsource, gown, (bprev0, bprev1), (back0, back1, back2), bextras)
    return attended, grad_q, grad_k, grad_v


def solution(mesh):
    tokens = P(("seq", "head"), None)
    return jax.shard_map(
        per_device,
        mesh=mesh,
        in_specs=(tokens,) * 4 + (P("seq", None),) * 2,
        out_specs=(tokens,) + (P("seq", "head"),) * 3,
        check_vma=False,
    )
```

time: 203 us -> 199 us (0.980)
  the two profiles are of different devices: /device:TPU:126 before, /device:TPU:32 now
where the time goes in v3:
time: 199 us; the launch traced here: 198 us
  waiting for transfers between devices  85.5 us (43%)
  starting transfers between devices  73.6 us (37%)
  Pallas kernels  34.4 us (17%)
    ppermute x13, waiting for transfers between devices, passed(): return lax.ppermute(shard, 'seq', pairs)  85.5 us
    ppermute x13, starting transfers between devices, passed(): return lax.ppermute(shard, 'seq', pairs)  31.3 us
    all_to_all x3, starting transfers between devices, spread(): return lax.all_to_all(x, 'head', split_axis=0, concat_axis=0)  28.7 us
    ppermute x6, starting transfers between devices, stepped(): return (lax.ppermute(shard, 'seq', pairs), source)  13.5 us
    pallas_call x1, Pallas kernels, attend(): pl.pallas_call(attend_body, out_shape=[jax.ShapeDtypeStruct((4, BLOCK, co...  12.4 us
    pallas_call x1, Pallas kernels, own_grads(): pl.pallas_call(own_body, out_shape=[jax.ShapeDtypeStruct((rows, cols), jn...  7 us
    pallas_call x2, Pallas kernels, pack_pair(): pl.pallas_call(pack_body, out_shape=jax.ShapeDtypeStruct((parts, 2, rows,...  6.82 us
    pallas_call x1, Pallas kernels, total(): pl.pallas_call(total_body, out_shape=[out, out], grid_spec=pltpu.Prefetch...  4.62 us
  transfers between devices with their start and end apart: 22, of which 8 were waited for; matrix products, arithmetic and copies ran while one was open for 1% of the time, Pallas kernels for 7%

profile of v3, /device:TPU:32, one launch (start us, length us, event | category | flops | bytes accessed | tf_op | source)
XLA Modules:
  0.0 198.1 jit_solution(14868335418773144507)
XLA Ops:
  0.6 0.0 copy-start.12
  0.6 3.4 %pack_pair.3 = bf16[4,2,64,1024]{3,2,1,0:T(8,128)(2,1)} custom-call(bf16[64,4096]{1,0:T(8,128)(2,1)} %a_ref.3, bf16[64,4096]{1,0:T(8,128)(2,1)} %b_ref.3), custom_call_target="tpu_custom_call" | custom-call | tf_op jit(solution)/shard_map/pack_pair/pallas_call | solution.py:63
  4.1 5.3 %all-to-all-start.1 = ((bf16[4,2,64,1024]{3,2,1,0:T(8,128)(2,1)}), bf16[4,2,64,1024]{3,2,1,0:T(8,128)(2,1)S(1)}, u32[]{:S(2)}, u32[]{:S(2)}) async-start(bf16[4,2,64,1024]{3,2,1,0:T(8,128)(2,1)} %pack_pair.3), calls=%async_computation.1 | async-start | bytes 2097152 | tf_op jit(solution)/shard_map/all_to_all | solution.py:351
  9.4 0.1 copy.13
  9.5 0.1 copy.12
  9.6 0.1 pad_add_fusion.used_ref
  9.7 1.3 collective-permute-start
  10.9 1.3 collective-permute-start.2
  12.2 1.3 collective-permute-start.1
  13.5 3.4 %pack_pair.2 = bf16[4,2,64,1024]{3,2,1,0:T(8,128)(2,1)} custom-call(bf16[64,4096]{1,0:T(8,128)(2,1)} %a_ref.2, bf16[64,4096]{1,0:T(8,128)(2,1)} %b_ref.2), custom_call_target="tpu_custom_call" | custom-call | tf_op jit(solution)/shard_map/pack_pair/pallas_call | solution.py:63
  17.0 10.3 %collective-permute-done.2 = s32[2]{0:T(128)S(1)} collective-permute-done((s32[2]{0:T(128)S(1)}, s32[2]{0:T(128)S(1)}, u32[]{:S(2)}, u32[]{:S(2)}) %collective-permute-start.2) | collective-permute-done | bytes 40 | tf_op jit(solution)/shard_map/ppermute | solution.py:39
  27.3 0.0 collective-permute-done.1
  27.3 0.6 pad_add_fusion.1.idx_ref
  27.9 0.0 all-to-all-done.1.kv_ref.own_ref
  27.9 3.8 %all-to-all-start = ((bf16[4,2,64,1024]{3,2,1,0:T(8,128)(2,1)}), bf16[4,2,64,1024]{3,2,1,0:T(8,128)(2,1)S(1)}, u32[]{:S(2)}, u32[]{:S(2)}) async-start(bf16[4,2,64,1024]{3,2,1,0:T(8,128)(2,1)} %pack_pair.2), calls=%async_computation | async-start | bytes 2097152 | tf_op jit(solution)/shard_map/all_to_all | solution.py:351
  31.7 3.5 %pick_blocks.1 = (bf16[2,2,64,1024]{3,2,1,0:T(8,128)(2,1)}, bf16[2,2,64,1024]{3,2,1,0:T(8,128)(2,1)}, bf16[2,2,64,1024]{3,2,1,0:T(8,128)(2,1)}, bf16[2,2,64,1024]{3,2,1,0:T(8,128)(2,1)}, bf16[2,2,64,1024]{3,2,1,0:T(8,128)(2,1)}) custom-call(s32[3,2]{1,0:T(4,128)} %pad_add_fusion.1.idx_ref, bf16[4,2,64,1024]{3,2,1,0:T(8,128)(2,1)} %copy-done), custom_call_target="tpu_custom_call" | custom-call | tf_op jit(solution)/shard_map/pick_blocks/pallas_call | solution.py:90
  35.3 3.5 %collective-permute-start.3 = (bf16[2,2,64,1024]{3,2,1,0:T(8,128)(2,1)}, bf16[2,2,64,1024]{3,2,1,0:T(8,128)(2,1)S(1)}, u32[]{:S(2)}, u32[]{:S(2)}) collective-permute-start(bf16[2,2,64,1024]{3,2,1,0:T(8,128)(2,1)} %get-tuple-element.25), channel_id=1, source_target_pairs={{0,4},{4,8},{8,12},{12,16},{16,20},{20,24},{24,28},{28,32},{32,36}... | collective-permute-start | bytes 1572872 | tf_op jit(solution)/shard_map/ppermute | solution.py:39
  38.7 4.8 %collective-permute-start.5 = (bf16[2,2,64,1024]{3,2,1,0:T(8,128)(2,1)}, bf16[2,2,64,1024]{3,2,1,0:T(8,128)(2,1)S(1)}, u32[]{:S(2)}, u32[]{:S(2)}) collective-permute-start(bf16[2,2,64,1024]{3,2,1,0:T(8,128)(2,1)} %get-tuple-element.27), channel_id=1, source_target_pairs={{0,8},{4,12},{8,16},{12,20},{16,24},{20,28},{24,32},{28,36},{32,40... | collective-permute-start | bytes 1572872 | tf_op jit(solution)/shard_map/ppermute | solution.py:39
  43.6 4.9 %collective-permute-start.6 = (bf16[2,2,64,1024]{3,2,1,0:T(8,128)(2,1)}, bf16[2,2,64,1024]{3,2,1,0:T(8,128)(2,1)S(1)}, u32[]{:S(2)}, u32[]{:S(2)}) collective-permute-start(bf16[2,2,64,1024]{3,2,1,0:T(8,128)(2,1)} %get-tuple-element.28), channel_id=1, source_target_pairs={{0,32},{4,36},{8,40},{12,44},{16,48},{20,52},{24,56},{28,60},{32,6... | collective-permute-start | bytes 1572872 | tf_op jit(solution)/shard_map/ppermute | solution.py:39
  48.5 2.2 %collective-permute-start.4 = (bf16[2,2,64,1024]{3,2,1,0:T(8,128)(2,1)}, bf16[2,2,64,1024]{3,2,1,0:T(8,128)(2,1)S(1)}, u32[]{:S(2)}, u32[]{:S(2)}) collective-permute-start(bf16[2,2,64,1024]{3,2,1,0:T(8,128)(2,1)} %get-tuple-element.26), channel_id=1, source_target_pairs={{0,4},{4,8},{8,12},{12,16},{16,20},{20,24},{24,28},{28,32},{32,36}... | collective-permute-start | bytes 1572872 | tf_op jit(solution)/shard_map/ppermute | solution.py:39
  50.7 5.6 %collective-permute-start.7 = (bf16[2,2,64,1024]{3,2,1,0:T(8,128)(2,1)}, bf16[2,2,64,1024]{3,2,1,0:T(8,128)(2,1)}, u32[]{:S(2)}, u32[]{:S(2)}) collective-permute-start(bf16[2,2,64,1024]{3,2,1,0:T(8,128)(2,1)} %get-tuple-element.29), channel_id=1, source_target_pairs={{0,128},{4,132},{8,136},{12,140},{16,144},{20,148},{24,152},{28,15... | collective-permute-start | bytes 1572872 | tf_op jit(solution)/shard_map/ppermute | solution.py:39
  56.3 6.3 %collective-permute-start.8 = (bf16[2,2,64,1024]{3,2,1,0:T(8,128)(2,1)S(1)}, bf16[2,2,64,1024]{3,2,1,0:T(8,128)(2,1)}, u32[]{:S(2)}, u32[]{:S(2)}) collective-permute-start(bf16[2,2,64,1024]{3,2,1,0:T(8,128)(2,1)S(1)} %collective-permute-done.3.prev0_ref), channel_id=1, source_target_pairs={{0,64},{64,128},{128,192},{1,65},{65,129},{129,193},{2,66},{66,130... | collective-permute-start | bytes 1572872 | tf_op jit(solution)/shard_map/ppermute | solution.py:52
  62.6 0.1 collective-permute-done.5.far0_ref
  62.6 1.4 collective-permute-start.9
  64.1 1.4 collective-permute-start.10
  65.5 0.7 pad_add_fusion.2.from_ref
  66.2 6.8 %collective-permute-done.4.prev1_ref = bf16[2,2,64,1024]{3,2,1,0:T(8,128)(2,1)S(1)} collective-permute-done((bf16[2,2,64,1024]{3,2,1,0:T(8,128)(2,1)}, bf16[2,2,64,1024]{3,2,1,0:T(8,128)(2,1)S(1)}, u32[]{:S(2)}, u32[]{:S(2)}) %collective-permute-start.4) | collective-permute-done | bytes 524320 | tf_op jit(solution)/shard_map/ppermute | solution.py:39
  73.0 4.1 %collective-permute-done.7.far2_ref = bf16[2,2,64,1024]{3,2,1,0:T(8,128)(2,1)} collective-permute-done((bf16[2,2,64,1024]{3,2,1,0:T(8,128)(2,1)}, bf16[2,2,64,1024]{3,2,1,0:T(8,128)(2,1)}, u32[]{:S(2)}, u32[]{:S(2)}) %collective-permute-start.7) | collective-permute-done | bytes 524320 | tf_op jit(solution)/shard_map/ppermute | solution.py:39
  77.2 0.0 collective-permute-done.8.rest_0_
  77.2 12.4 %attend.1 = (bf16[4,64,1024]{2,1,0:T(8,128)(2,1)}, bf16[8,256,896]{2,1,0:T(8,128)(2,1)}, bf16[8,256,256]{2,1,0:T(8,128)(2,1)}, bf16[2,2,64,1024]{3,2,1,0:T(8,128...) custom-call(s32[1]{0:T(128)} %bitcast.span_ref, ...), custom_call_target="tpu_custom_call" | custom-call | tf_op jit(solution)/shard_map/attend/pallas_call | solution.py:216
  89.7 1.3 collective-permute-start.11
  91.0 1.3 collective-permute-start.13
  92.3 1.3 collective-permute-start.14
  93.6 19.6 %all-to-all-start.2 = ((bf16[4,64,1024]{2,1,0:T(8,128)(2,1)}), bf16[4,64,1024]{2,1,0:T(8,128)(2,1)S(1)}, u32[]{:S(2)}, u32[]{:S(2)}) async-start(bf16[4,64,1024]{2,1,0:T(8,128)(2,1)} %get-tuple-element.30), calls=%async_computation.2 | async-start | bytes 1048576 | tf_op jit(solution)/shard_map/all_to_all | solution.py:351
  113.1 1.3 collective-permute-start.12
  114.4 1.3 collective-permute-start.15
  115.7 9.2 %collective-permute-done.11.gprev0_ref = bf16[2,2,64,1024]{3,2,1,0:T(8,128)(2,1)S(1)} collective-permute-done((bf16[2,2,64,1024]{3,2,1,0:T(8,128)(2,1)}, bf16[2,2,64,1024]{3,2,1,0:T(8,128)(2,1)S(1)}, u32[]{:S(2)}, u32[]{:S(2)}) %collective-permute-start.11) | collective-permute-done | bytes 524320 | tf_op jit(solution)/shard_map/ppermute | solution.py:39
  124.9 1.5 collective-permute-start.16
  126.3 1.4 collective-permute-start.17
  127.8 0.3 collective-permute-done.14.gfar1_ref
  128.1 1.5 collective-permute-start.18
  129.5 0.6 pad_add_fusion.3.from_ref
  130.1 7.0 %own_grads.1 = (bf16[256,1024]{1,0:T(8,128)(2,1)}, f32[2,256,1024]{2,1,0:T(8,128)}) custom-call(s32[3]{0:T(128)} %pad_add_fusion.2.from_ref, bf16[4,2,64,1024]{3,2,1,0:T(8,128)(2,1)} %copy-done.1, bf16[4,2,64,1024]{3,2,1,0:T(8,128)(2,1)} %copy-done, bf16[2,2,64,1024]{3,2,1,0:T(8,128)(2,1)} %copy-done.2, bf16[2,2,64,1024]{3,2,1,0:T(8,128)(2,1)} %copy-done.5, ...), custom_call_target="tpu_custom_call" | custom-call | tf_op jit(solution)/shard_map/own_grads/pallas_call | solution.py:281
  137.1 0.8 copy.15
  138.0 5.0 %collective-permute-done.12.gprev1_ref = bf16[2,2,64,1024]{3,2,1,0:T(8,128)(2,1)S(1)} collective-permute-done((bf16[2,2,64,1024]{3,2,1,0:T(8,128)(2,1)}, bf16[2,2,64,1024]{3,2,1,0:T(8,128)(2,1)S(1)}, u32[]{:S(2)}, u32[]{:S(2)}) %collective-permute-start.12) | collective-permute-done | bytes 524320 | tf_op jit(solution)/shard_map/ppermute | solution.py:39
  143.0 49.7 %collective-permute-done.15.gfar2_ref = bf16[2,2,64,1024]{3,2,1,0:T(8,128)(2,1)S(1)} collective-permute-done((bf16[2,2,64,1024]{3,2,1,0:T(8,128)(2,1)}, bf16[2,2,64,1024]{3,2,1,0:T(8,128)(2,1)S(1)}, u32[]{:S(2)}, u32[]{:S(2)}) %collective-permute-start.15) | collective-permute-done | bytes 524320 | tf_op jit(solution)/shard_map/ppermute | solution.py:39
  192.7 0.8 copy-done.10
  193.5 4.6 %total.1 = (bf16[256,1024]{1,0:T(8,128)(2,1)}, bf16[256,1024]{1,0:T(8,128)(2,1)}) custom-call(s32[3,2]{1,0:T(4,128)} %pad_add_fusion.1.idx_ref, s32[3]{0:T(128)} %pad_add_fusion.3.from_ref, f32[2,256,1024]{2,1,0:T(8,128)} %get-tuple-element.34.gown_ref, bf16[2,2,64,1024]{3,2,1,0:T(8,128)(2,1)} %copy-done.6, bf16[2,2,64,1024]{3,2,1,0:T(8,128)(2,1)} %copy-done.9, ...), custom_call_target="tpu_custom_call" | custom-call | tf_op jit(solution)/shard_map/total/pallas_call | solution.py:336
  (37 shorter events, 0.1 us)
Async XLA Ops:
  0.6 8.7 %copy-start.12 = (s32[4,3]{1,0:T(4,128)S(1)}, s32[4,3]{1,0:T(4,128)}, u32[]{:S(2)}) copy-start(s32[4,3]{1,0:T(4,128)} %lists_ref.1) | copy-start | bytes 148
  4.1 23.8 %all-to-all-start.1 = ((bf16[4,2,64,1024]{3,2,1,0:T(8,128)(2,1)}), bf16[4,2,64,1024]{3,2,1,0:T(8,128)(2,1)S(1)}, u32[]{:S(2)}, u32[]{:S(2)}) async-start(bf16[4,2,64,1024]{3,2,1,0:T(8,128)(2,1)} %pack_pair.3), calls=%async_computation.1 | async-start | bytes 2097152 | tf_op jit(solution)/shard_map/all_to_all | solution.py:351
  9.6 67.5 %copy-start.11 = (s32[3,2]{1,0:T(4,128)}, s32[3,2]{1,0:T(4,128)S(1)}, u32[]{:S(2)}) copy-start(s32[3,2]{1,0:T(4,128)S(1)} %pad_add_fusion.used_ref) | copy-start | bytes 76
  9.7 7.3 %collective-permute-start = (s32[2]{0:T(128)S(1)}, s32[2]{0:T(128)S(1)}, u32[]{:S(2)}, u32[]{:S(2)}) collective-permute-start(s32[2]{0:T(128)S(1)} %get-tuple-element.44), channel_id=1, source_target_pairs={{252,244},{248,240},{244,236},{240,232},{236,228},{232,224},{228,2... | collective-permute-start | bytes 32 | tf_op jit(solution)/shard_map/ppermute | solution.py:39
  10.9 16.3 %collective-permute-start.2 = (s32[2]{0:T(128)S(1)}, s32[2]{0:T(128)S(1)}, u32[]{:S(2)}, u32[]{:S(2)}) collective-permute-start(s32[2]{0:T(128)S(1)} %get-tuple-element.45), channel_id=1, source_target_pairs={{252,124},{248,120},{244,116},{240,112},{236,108},{232,104},{228,1... | collective-permute-start | bytes 32 | tf_op jit(solution)/shard_map/ppermute | solution.py:39
  12.2 15.0 %collective-permute-start.1 = (s32[2]{0:T(128)S(1)}, s32[2]{0:T(128)S(1)}, u32[]{:S(2)}, u32[]{:S(2)}) collective-permute-start(s32[2]{0:T(128)S(1)} %get-tuple-element.46), channel_id=1, source_target_pairs={{252,220},{248,216},{244,212},{240,208},{236,204},{232,200},{228,1... | collective-permute-start | bytes 32 | tf_op jit(solution)/shard_map/ppermute | solution.py:39
  27.9 3.9 %copy-start = (bf16[4,2,64,1024]{3,2,1,0:T(8,128)(2,1)}, bf16[4,2,64,1024]{3,2,1,0:T(8,128)(2,1)S(1)}, u32[]{:S(2)}) copy-start(bf16[4,2,64,1024]{3,2,1,0:T(8,128)(2,1)S(1)} %all-to-all-done.1.kv_ref.own_ref) | copy-start | bytes 3145732
  27.9 38.3 %all-to-all-start = ((bf16[4,2,64,1024]{3,2,1,0:T(8,128)(2,1)}), bf16[4,2,64,1024]{3,2,1,0:T(8,128)(2,1)S(1)}, u32[]{:S(2)}, u32[]{:S(2)}) async-start(bf16[4,2,64,1024]{3,2,1,0:T(8,128)(2,1)} %pack_pair.2), calls=%async_computation | async-start | bytes 2097152 | tf_op jit(solution)/shard_map/all_to_all | solution.py:351
  35.3 21.1 %collective-permute-start.3 = (bf16[2,2,64,1024]{3,2,1,0:T(8,128)(2,1)}, bf16[2,2,64,1024]{3,2,1,0:T(8,128)(2,1)S(1)}, u32[]{:S(2)}, u32[]{:S(2)}) collective-permute-start(bf16[2,2,64,1024]{3,2,1,0:T(8,128)(2,1)} %get-tuple-element.25), channel_id=1, source_target_pairs={{0,4},{4,8},{8,12},{12,16},{16,20},{20,24},{24,28},{28,32},{32,36}... | collective-permute-start | bytes 1572872 | tf_op jit(solution)/shard_map/ppermute | solution.py:39
  38.7 23.9 %collective-permute-start.5 = (bf16[2,2,64,1024]{3,2,1,0:T(8,128)(2,1)}, bf16[2,2,64,1024]{3,2,1,0:T(8,128)(2,1)S(1)}, u32[]{:S(2)}, u32[]{:S(2)}) collective-permute-start(bf16[2,2,64,1024]{3,2,1,0:T(8,128)(2,1)} %get-tuple-element.27), channel_id=1, source_target_pairs={{0,8},{4,12},{8,16},{12,20},{16,24},{20,28},{24,32},{28,36},{32,40... | collective-permute-start | bytes 1572872 | tf_op jit(solution)/shard_map/ppermute | solution.py:39
  43.6 20.5 %collective-permute-start.6 = (bf16[2,2,64,1024]{3,2,1,0:T(8,128)(2,1)}, bf16[2,2,64,1024]{3,2,1,0:T(8,128)(2,1)S(1)}, u32[]{:S(2)}, u32[]{:S(2)}) collective-permute-start(bf16[2,2,64,1024]{3,2,1,0:T(8,128)(2,1)} %get-tuple-element.28), channel_id=1, source_target_pairs={{0,32},{4,36},{8,40},{12,44},{16,48},{20,52},{24,56},{28,60},{32,6... | collective-permute-start | bytes 1572872 | tf_op jit(solution)/shard_map/ppermute | solution.py:39
  48.5 24.5 %collective-permute-start.4 = (bf16[2,2,64,1024]{3,2,1,0:T(8,128)(2,1)}, bf16[2,2,64,1024]{3,2,1,0:T(8,128)(2,1)S(1)}, u32[]{:S(2)}, u32[]{:S(2)}) collective-permute-start(bf16[2,2,64,1024]{3,2,1,0:T(8,128)(2,1)} %get-tuple-element.26), channel_id=1, source_target_pairs={{0,4},{4,8},{8,12},{12,16},{16,20},{20,24},{24,28},{28,32},{32,36}... | collective-permute-start | bytes 1572872 | tf_op jit(solution)/shard_map/ppermute | solution.py:39
  50.7 26.4 %collective-permute-start.7 = (bf16[2,2,64,1024]{3,2,1,0:T(8,128)(2,1)}, bf16[2,2,64,1024]{3,2,1,0:T(8,128)(2,1)}, u32[]{:S(2)}, u32[]{:S(2)}) collective-permute-start(bf16[2,2,64,1024]{3,2,1,0:T(8,128)(2,1)} %get-tuple-element.29), channel_id=1, source_target_pairs={{0,128},{4,132},{8,136},{12,140},{16,144},{20,148},{24,152},{28,15... | collective-permute-start | bytes 1572872 | tf_op jit(solution)/shard_map/ppermute | solution.py:39
  56.3 20.9 %copy-start.2 = (bf16[2,2,64,1024]{3,2,1,0:T(8,128)(2,1)}, bf16[2,2,64,1024]{3,2,1,0:T(8,128)(2,1)S(1)}, u32[]{:S(2)}) copy-start(bf16[2,2,64,1024]{3,2,1,0:T(8,128)(2,1)S(1)} %collective-permute-done.3.prev0_ref) | copy-start | bytes 1572868
  56.3 20.9 %collective-permute-start.8 = (bf16[2,2,64,1024]{3,2,1,0:T(8,128)(2,1)S(1)}, bf16[2,2,64,1024]{3,2,1,0:T(8,128)(2,1)}, u32[]{:S(2)}, u32[]{:S(2)}) collective-permute-start(bf16[2,2,64,1024]{3,2,1,0:T(8,128)(2,1)S(1)} %collective-permute-done.3.prev0_ref), channel_id=1, source_target_pairs={{0,64},{64,128},{128,192},{1,65},{65,129},{129,193},{2,66},{66,130... | collective-permute-start | bytes 1572872 | tf_op jit(solution)/shard_map/ppermute | solution.py:52
  62.6 14.6 %copy-start.3 = (bf16[2,2,64,1024]{3,2,1,0:T(8,128)(2,1)}, bf16[2,2,64,1024]{3,2,1,0:T(8,128)(2,1)S(1)}, u32[]{:S(2)}) copy-start(bf16[2,2,64,1024]{3,2,1,0:T(8,128)(2,1)S(1)} %collective-permute-done.5.far0_ref) | copy-start | bytes 1572868
  62.6 14.5 %collective-permute-start.9 = (bf16[2,2,64,1024]{3,2,1,0:T(8,128)(2,1)S(1)}, bf16[2,2,64,1024]{3,2,1,0:T(8,128)(2,1)}, u32[]{:S(2)}, u32[]{:S(2)}) collective-permute-start(bf16[2,2,64,1024]{3,2,1,0:T(8,128)(2,1)S(1)} %collective-permute-done.5.far0_ref), channel_id=1, source_target_pairs={{4,68},{68,132},{132,196},{5,69},{69,133},{133,197},{6,70},{70,134... | collective-permute-start | bytes 1572872 | tf_op jit(solution)/shard_map/ppermute | solution.py:52
  64.1 13.1 %copy-start.4 = (bf16[2,2,64,1024]{3,2,1,0:T(8,128)(2,1)}, bf16[2,2,64,1024]{3,2,1,0:T(8,128)(2,1)S(1)}, u32[]{:S(2)}) copy-start(bf16[2,2,64,1024]{3,2,1,0:T(8,128)(2,1)S(1)} %collective-permute-done.6.far1_ref) | copy-start | bytes 1572868
  64.1 13.1 %collective-permute-start.10 = (bf16[2,2,64,1024]{3,2,1,0:T(8,128)(2,1)S(1)}, bf16[2,2,64,1024]{3,2,1,0:T(8,128)(2,1)}, u32[]{:S(2)}, u32[]{:S(2)}) collective-permute-start(bf16[2,2,64,1024]{3,2,1,0:T(8,128)(2,1)S(1)} %collective-permute-done.6.far1_ref), channel_id=1, source_target_pairs={{24,88},{28,92},{88,152},{92,156},{152,216},{156,220},{25,89},{29,... | collective-permute-start | bytes 1572872 | tf_op jit(solution)/shard_map/ppermute | solution.py:52
  66.2 11.0 %copy-start.1 = (bf16[4,2,64,1024]{3,2,1,0:T(8,128)(2,1)}, bf16[4,2,64,1024]{3,2,1,0:T(8,128)(2,1)S(1)}, u32[]{:S(2)}) copy-start(bf16[4,2,64,1024]{3,2,1,0:T(8,128)(2,1)S(1)} %all-to-all-done.qd_ref) | copy-start | bytes 3145732
  73.0 4.2 %copy-start.5 = (bf16[2,2,64,1024]{3,2,1,0:T(8,128)(2,1)}, bf16[2,2,64,1024]{3,2,1,0:T(8,128)(2,1)S(1)}, u32[]{:S(2)}) copy-start(bf16[2,2,64,1024]{3,2,1,0:T(8,128)(2,1)S(1)} %collective-permute-done.4.prev1_ref) | copy-start | bytes 1572868
  89.7 35.2 %collective-permute-start.11 = (bf16[2,2,64,1024]{3,2,1,0:T(8,128)(2,1)}, bf16[2,2,64,1024]{3,2,1,0:T(8,128)(2,1)S(1)}, u32[]{:S(2)}, u32[]{:S(2)}) collective-permute-start(bf16[2,2,64,1024]{3,2,1,0:T(8,128)(2,1)} %get-tuple-element.35), channel_id=1, source_target_pairs={{252,248},{248,244},{244,240},{240,236},{236,232},{232,228},{228,2... | collective-permute-start | bytes 1572872 | tf_op jit(solution)/shard_map/ppermute | solution.py:39
  91.0 35.4 %collective-permute-start.13 = (bf16[2,2,64,1024]{3,2,1,0:T(8,128)(2,1)}, bf16[2,2,64,1024]{3,2,1,0:T(8,128)(2,1)S(1)}, u32[]{:S(2)}, u32[]{:S(2)}) collective-permute-start(bf16[2,2,64,1024]{3,2,1,0:T(8,128)(2,1)} %get-tuple-element.37), channel_id=1, source_target_pairs={{252,244},{248,240},{244,236},{240,232},{236,228},{232,224},{228,2... | collective-permute-start | bytes 1572872 | tf_op jit(solution)/shard_map/ppermute | solution.py:39
  92.3 35.8 %collective-permute-start.14 = (bf16[2,2,64,1024]{3,2,1,0:T(8,128)(2,1)}, bf16[2,2,64,1024]{3,2,1,0:T(8,128)(2,1)S(1)}, u32[]{:S(2)}, u32[]{:S(2)}) collective-permute-start(bf16[2,2,64,1024]{3,2,1,0:T(8,128)(2,1)} %get-tuple-element.38), channel_id=1, source_target_pairs={{252,220},{248,216},{244,212},{240,208},{236,204},{232,200},{228,1... | collective-permute-start | bytes 1572872 | tf_op jit(solution)/shard_map/ppermute | solution.py:39
  93.6 43.6 %all-to-all-start.2 = ((bf16[4,64,1024]{2,1,0:T(8,128)(2,1)}), bf16[4,64,1024]{2,1,0:T(8,128)(2,1)S(1)}, u32[]{:S(2)}, u32[]{:S(2)}) async-start(bf16[4,64,1024]{2,1,0:T(8,128)(2,1)} %get-tuple-element.30), calls=%async_computation.2 | async-start | bytes 1048576 | tf_op jit(solution)/shard_map/all_to_all | solution.py:351
  113.1 29.9 %collective-permute-start.12 = (bf16[2,2,64,1024]{3,2,1,0:T(8,128)(2,1)}, bf16[2,2,64,1024]{3,2,1,0:T(8,128)(2,1)S(1)}, u32[]{:S(2)}, u32[]{:S(2)}) collective-permute-start(bf16[2,2,64,1024]{3,2,1,0:T(8,128)(2,1)} %get-tuple-element.36), channel_id=1, source_target_pairs={{252,248},{248,244},{244,240},{240,236},{236,232},{232,228},{228,2... | collective-permute-start | bytes 1572872 | tf_op jit(solution)/shard_map/ppermute | solution.py:39
  114.4 78.3 %collective-permute-start.15 = (bf16[2,2,64,1024]{3,2,1,0:T(8,128)(2,1)}, bf16[2,2,64,1024]{3,2,1,0:T(8,128)(2,1)S(1)}, u32[]{:S(2)}, u32[]{:S(2)}) collective-permute-start(bf16[2,2,64,1024]{3,2,1,0:T(8,128)(2,1)} %get-tuple-element.39), channel_id=1, source_target_pairs={{252,124},{248,120},{244,116},{240,112},{236,108},{232,104},{228,1... | collective-permute-start | bytes 1572872 | tf_op jit(solution)/shard_map/ppermute | solution.py:39
  124.9 12.2 %copy-start.6 = (bf16[2,2,64,1024]{3,2,1,0:T(8,128)(2,1)}, bf16[2,2,64,1024]{3,2,1,0:T(8,128)(2,1)S(1)}, u32[]{:S(2)}) copy-start(bf16[2,2,64,1024]{3,2,1,0:T(8,128)(2,1)S(1)} %collective-permute-done.11.gprev0_ref) | copy-start | bytes 1572868
  124.9 67.8 %collective-permute-start.16 = (bf16[2,2,64,1024]{3,2,1,0:T(8,128)(2,1)S(1)}, bf16[2,2,64,1024]{3,2,1,0:T(8,128)(2,1)}, u32[]{:S(2)}, u32[]{:S(2)}) collective-permute-start(bf16[2,2,64,1024]{3,2,1,0:T(8,128)(2,1)S(1)} %collective-permute-done.11.gprev0_ref), channel_id=1, source_target_pairs={{252,188},{188,124},{124,60},{253,189},{189,125},{125,61},{254,190... | collective-permute-start | bytes 1572872 | tf_op jit(solution)/shard_map/ppermute | solution.py:52
  126.3 10.8 %copy-start.7 = (bf16[2,2,64,1024]{3,2,1,0:T(8,128)(2,1)}, bf16[2,2,64,1024]{3,2,1,0:T(8,128)(2,1)S(1)}, u32[]{:S(2)}) copy-start(bf16[2,2,64,1024]{3,2,1,0:T(8,128)(2,1)S(1)} %collective-permute-done.13.gfar0_ref) | copy-start | bytes 1572868
  126.3 66.4 %collective-permute-start.17 = (bf16[2,2,64,1024]{3,2,1,0:T(8,128)(2,1)S(1)}, bf16[2,2,64,1024]{3,2,1,0:T(8,128)(2,1)}, u32[]{:S(2)}, u32[]{:S(2)}) collective-permute-start(bf16[2,2,64,1024]{3,2,1,0:T(8,128)(2,1)S(1)} %collective-permute-done.13.gfar0_ref), channel_id=1, source_target_pairs={{248,184},{184,120},{120,56},{249,185},{185,121},{121,57},{250,186... | collective-permute-start | bytes 1572872 | tf_op jit(solution)/shard_map/ppermute | solution.py:52
  128.1 9.1 %copy-start.8 = (bf16[2,2,64,1024]{3,2,1,0:T(8,128)(2,1)}, bf16[2,2,64,1024]{3,2,1,0:T(8,128)(2,1)S(1)}, u32[]{:S(2)}) copy-start(bf16[2,2,64,1024]{3,2,1,0:T(8,128)(2,1)S(1)} %collective-permute-done.14.gfar1_ref) | copy-start | bytes 1572868
  128.1 64.6 %collective-permute-start.18 = (bf16[2,2,64,1024]{3,2,1,0:T(8,128)(2,1)S(1)}, bf16[2,2,64,1024]{3,2,1,0:T(8,128)(2,1)}, u32[]{:S(2)}, u32[]{:S(2)}) collective-permute-start(bf16[2,2,64,1024]{3,2,1,0:T(8,128)(2,1)S(1)} %collective-permute-done.14.gfar1_ref), channel_id=1, source_target_pairs={{228,164},{224,160},{164,100},{160,96},{100,36},{96,32},{229,165},... | collective-permute-start | bytes 1572872 | tf_op jit(solution)/shard_map/ppermute | solution.py:52
  143.0 49.7 %copy-start.9 = (bf16[2,2,64,1024]{3,2,1,0:T(8,128)(2,1)}, bf16[2,2,64,1024]{3,2,1,0:T(8,128)(2,1)S(1)}, u32[]{:S(2)}) copy-start(bf16[2,2,64,1024]{3,2,1,0:T(8,128)(2,1)S(1)} %collective-permute-done.12.gprev1_ref) | copy-start | bytes 1572868
  192.7 0.8 copy-start.10
